TPU v7x, 128 devices: a whole 4x4x4 slice. The times are simulated.
128 devices in a mesh: ctx: 32 (over z, y, core), head: 2 (over x_lo), section: 2 (over x_hi).
Axes of the slice: x: 4 (x_hi: 2, x_lo: 2; x = x_hi * 2 + x_lo), y: 4, z: 4, core: 2. Of those that a mesh axis runs over, the one named last changes fastest.
Arguments:
- delta_query: bfloat16 [2, 4096, 2048], P('section', 'ctx', 'head'), may hold values from -6 to 6
- delta_key: bfloat16 [2, 4096, 2048], P('section', 'ctx', 'head'), may hold values from -6 to 6
- delta_value: bfloat16 [2, 4096, 2048], P('section', 'ctx', 'head'), may hold values from -6 to 6
- beta_logit: float32 [2, 4096, 16], P('section', 'ctx', 'head'), may hold values from -6 to 6
- decay_input: float32 [2, 4096, 16], P('section', 'ctx', 'head'), may hold values from -4 to 36864
- decay_log: float32 [16], P('head'), may hold values from -14 to -2
- norm_gain: float32 [128], replicated, may hold values from 0.25 to 1.75
- output_gate: bfloat16 [2, 4096, 2048], P('section', 'ctx', 'head'), may hold values from -6 to 6
- delta_cotangent: bfloat16 [2, 4096, 2048], P('section', 'ctx', 'head'), may hold values from -12 to 12
- attn_query: bfloat16 [2, 4096, 4096], P('section', 'ctx', 'head'), may hold values from -5 to 5
- attn_key: bfloat16 [2, 4096, 512], P('section', 'ctx', 'head'), may hold values from -5 to 5
- attn_value: bfloat16 [2, 4096, 512], P('section', 'ctx', 'head'), may hold values from -6 to 6
- attn_gate: bfloat16 [2, 4096, 4096], P('section', 'ctx', 'head'), may hold values from -6 to 6
- attn_cotangent: bfloat16 [2, 4096, 4096], P('section', 'ctx', 'head'), may hold values from -6 to 6
Outputs:
- delta_output: bfloat16 [2, 4096, 2048], P('section', 'ctx', 'head')
- grad_delta_query: bfloat16 [2, 4096, 2048], P('section', 'ctx', 'head')
- grad_delta_key: bfloat16 [2, 4096, 2048], P('section', 'ctx', 'head')
- grad_delta_value: bfloat16 [2, 4096, 2048], P('section', 'ctx', 'head')
- grad_beta_logit: float32 [2, 4096, 16], P('section', 'ctx', 'head')
- grad_decay_input: float32 [2, 4096, 16], P('section', 'ctx', 'head')
- grad_decay_log: float32 [16], P('head')
- grad_norm_gain: float32 [128], replicated
- grad_output_gate: bfloat16 [2, 4096, 2048], P('section', 'ctx', 'head')
- attn_output: bfloat16 [2, 4096, 4096], P('section', 'ctx', 'head')
- grad_attn_query: bfloat16 [2, 4096, 4096], P('section', 'ctx', 'head')
- grad_attn_key: bfloat16 [2, 4096, 512], P('section', 'ctx', 'head')
- grad_attn_value: bfloat16 [2, 4096, 512], P('section', 'ctx', 'head')
- grad_attn_gate: bfloat16 [2, 4096, 4096], P('section', 'ctx', 'head')
All inputs are finite; a program needn't handle non-finite values.
Results may differ from a plain program's by a relative error of at most 0.02.
Values may be sent and summed in bfloat16 or wider, within the bound.
A program may use at most 256 MiB of HBM per device.

v0:
```python
import jax
import jax.numpy as jnp
from jax import lax
from jax.sharding import PartitionSpec as P

BLOCK_LEN = 64
AD = 256


HIGHEST = lax.Precision.HIGHEST
NEG_FILL = -1e30


def passed_along(block, axis, distance):
    devices = range(lax.axis_size(axis))
    route = [(i - distance, i) for i in devices if i - distance in devices]
    return lax.ppermute(block, axis, route)


def carried_in(value, axis, combine, identity):
    count, here = (lax.axis_size(axis), lax.axis_index(axis))
    everything = jax.tree.map(lambda part: lax.all_gather(part, axis), value)
    start = jax.tree.map(
        lambda part, zero: jnp.broadcast_to(jnp.asarray(zero, part.dtype), part.shape),
        value,
        identity,
    )

    def lap(k, before):
        at = count - 1 - k
        reached = at > here
        new = combine(before, jax.tree.map(lambda part: part[at], everything))
        return jax.tree.map(lambda a, b: jnp.where(reached, a, b), new, before)

    return lax.fori_loop(0, count, lap, start)


def unit_rows(values):
    return values * lax.rsqrt(jnp.sum(values * values, axis=-1, keepdims=True) + 1e-06)


def decay_inverse(lower_part):
    block_rows = lower_part.shape[-1]
    identity = jnp.eye(block_rows, dtype=jnp.float32)
    result = identity - lower_part
    powered = lower_part
    for doubling in range(block_rows.bit_length() - 2):
        powered = jnp.einsum("hij,hjk->hik", powered, powered, precision=HIGHEST)
        result = jnp.einsum("hij,hjk->hik", result, identity + powered, precision=HIGHEST)
    return result


def split_rows(array, block_rows):
    shaped = array.reshape((array.shape[0] // block_rows, block_rows) + array.shape[1:])
    return jnp.swapaxes(shaped, 1, 2)


def delta_inputs(queries, keys_in, beta_in, decay_in, decay_rates):
    scaling = queries.shape[-1] ** (-0.5)
    unit_queries = unit_rows(queries) * scaling
    unit_keys = unit_rows(keys_in)
    beta_values = jax.nn.sigmoid(beta_in)
    decays = -jnp.exp(decay_rates)[None, :] * jax.nn.softplus(decay_in)
    return (unit_queries, unit_keys, beta_values, decays)


def block_terms(keys_in, values, beta_values, decays):
    block_rows = decays.shape[1]
    cumulative = jnp.cumsum(decays, axis=1)
    row_ids = lax.broadcasted_iota(jnp.int32, (block_rows, block_rows), 0)
    col_ids = lax.broadcasted_iota(jnp.int32, (block_rows, block_rows), 1)
    strict = row_ids > col_ids
    within = row_ids >= col_ids
    spread = cumulative[:, :, None] - cumulative[:, None, :]
    fading = jnp.exp(jnp.where(within, spread, 0.0))
    products = jnp.einsum("hcd,hed->hce", keys_in, keys_in, precision=HIGHEST)
    lower_part = jnp.where(strict, beta_values[:, :, None] * fading * products, 0.0)
    solved = decay_inverse(lower_part)
    value_part = jnp.einsum(
        "hce,hev->hcv", solved, beta_values[:, :, None] * values, precision=HIGHEST
    )
    key_part = jnp.einsum(
        "hce,hed->hcd",
        solved,
        (beta_values * jnp.exp(cumulative))[:, :, None] * keys_in,
        precision=HIGHEST,
    )
    tail_decay = jnp.exp(cumulative[:, -1:] - cumulative)
    return (cumulative, fading, within, value_part, key_part, tail_decay)


def block_output(state, terms, queries, keys_in):
    cumulative, fading, within, value_part, key_part, tail_decay = terms
    update = value_part - jnp.einsum("hcd,hvd->hcv", key_part, state, precision=HIGHEST)
    scores = jnp.where(
        within, jnp.einsum("hcd,hed->hce", queries, keys_in, precision=HIGHEST) * fading, 0.0
    )
    carried = jnp.exp(cumulative)[:, :, None] * jnp.einsum(
        "hcd,hvd->hcv", queries, state, precision=HIGHEST
    )
    output = carried + jnp.einsum("hce,hev->hcv", scores, update, precision=HIGHEST)
    weighted = tail_decay[:, :, None] * keys_in
    state_next = jnp.exp(cumulative[:, -1])[:, None, None] * state + jnp.einsum(
        "hcv,hcd->hvd", update, weighted, precision=HIGHEST
    )
    return (output, state_next)


def block_map(keys_in, values, beta_values, decays):
    cumulative, fading, within, value_part, key_part, tail_decay = block_terms(
        keys_in, values, beta_values, decays
    )
    weighted = tail_decay[:, :, None] * keys_in
    head_size = keys_in.shape[-1]
    transfer = jnp.exp(cumulative[:, -1])[:, None, None] * jnp.eye(
        head_size, dtype=jnp.float32
    ) - jnp.einsum("hcd,hce->hde", key_part, weighted, precision=HIGHEST)
    offset = jnp.einsum("hcv,hce->hve", value_part, weighted, precision=HIGHEST)
    return (transfer, offset)


def compose(earlier, later):
    return (
        jnp.einsum("hij,hjk->hik", earlier[0], later[0], precision=HIGHEST),
        jnp.einsum("hij,hjk->hik", earlier[1], later[0], precision=HIGHEST) + later[1],
    )


def delta_layer(
    state,
    queries,
    keys_in,
    values,
    beta_in,
    decay_in,
    decay_rates,
    gain_in,
    gate_values,
    block_rows,
):
    unit_queries, unit_keys, beta_values, decays = delta_inputs(
        queries, keys_in, beta_in, decay_in, decay_rates
    )
    tokens, heads, head_size = queries.shape

    def advance(carried, pieces):
        block_queries, block_keys, block_values, block_betas, block_decays = pieces
        terms = block_terms(block_keys, block_values, block_betas, block_decays)
        output, carried_next = block_output(carried, terms, block_queries, block_keys)
        return (carried_next, output)

    pieces = (
        split_rows(unit_queries, block_rows),
        split_rows(unit_keys, block_rows),
        split_rows(values, block_rows),
        split_rows(beta_values, block_rows),
        split_rows(decays, block_rows),
    )
    state_end, outputs = lax.scan(advance, state, pieces)
    mixture = jnp.swapaxes(outputs, 1, 2).reshape(tokens, heads, head_size)
    normed = mixture * lax.rsqrt(jnp.mean(mixture * mixture, axis=-1, keepdims=True) + 1e-06)
    return (normed * gain_in * jax.nn.silu(gate_values), state_end)


def block_scores(queries, key_block, query_start, key_start):
    scores = jnp.einsum(
        "ikgd,jkd->kgij", queries, key_block, preferred_element_type=jnp.float32
    ) * queries.shape[-1] ** (-0.5)
    rows_at = query_start + lax.broadcasted_iota(
        jnp.int32, (queries.shape[0], key_block.shape[0]), 0
    )
    cols_at = key_start + lax.broadcasted_iota(jnp.int32, (queries.shape[0], key_block.shape[0]), 1)
    return jnp.where(cols_at <= rows_at, scores, NEG_FILL)


def key_blocks_of(keys_all, values_all):
    length = keys_all.shape[0]
    block_rows = min(512, length)
    block_count = length // block_rows
    key_blocks = keys_all.reshape((block_count, block_rows) + keys_all.shape[1:])
    value_blocks = values_all.reshape((block_count, block_rows) + values_all.shape[1:])
    starts = jnp.arange(block_count, dtype=jnp.int32) * block_rows
    return (key_blocks, value_blocks, starts)


def attend(queries, keys_all, values_all, query_start):
    key_blocks, value_blocks, starts = key_blocks_of(keys_all, values_all)
    stat_shape = (queries.shape[1], queries.shape[2], queries.shape[0])

    def gather_stats(carried, pieces):
        running_max, running_sum = carried
        key_block, key_start = pieces
        scores = block_scores(queries, key_block, query_start, key_start)
        new_max = jnp.maximum(running_max, jnp.max(scores, axis=-1))
        new_sum = running_sum * jnp.exp(running_max - new_max) + jnp.sum(
            jnp.exp(scores - new_max[..., None]), axis=-1
        )
        return ((new_max, new_sum), None)

    initial = (jnp.full(stat_shape, NEG_FILL, jnp.float32), jnp.zeros(stat_shape, jnp.float32))
    row_max, row_sum = lax.scan(gather_stats, initial, (key_blocks, starts))[0]
    log_total = row_max + jnp.log(row_sum)

    def weigh(running, pieces):
        key_block, value_block, key_start = pieces
        scores = block_scores(queries, key_block, query_start, key_start)
        weights = jnp.exp(scores - log_total[..., None]).astype(jnp.bfloat16)
        return (
            running
            + jnp.einsum(
                "kgij,jkd->ikgd", weights, value_block, preferred_element_type=jnp.float32
            ),
            None,
        )

    attended = lax.scan(
        weigh, jnp.zeros(queries.shape, jnp.float32), (key_blocks, value_blocks, starts)
    )[0]
    return (attended, log_total)


def key_block_grads(
    queries, key_block, value_block, query_start, key_start, log_total, upstream, centering
):
    scores = block_scores(queries, key_block, query_start, key_start)
    probs = jnp.exp(scores - log_total[..., None])
    weights = probs.astype(jnp.bfloat16)
    value_grad = jnp.einsum("kgij,ikgd->jkd", weights, upstream, preferred_element_type=jnp.float32)
    weight_grad = jnp.einsum(
        "ikgd,jkd->kgij", upstream, value_block, preferred_element_type=jnp.float32
    )
    score_grad = (probs * (weight_grad - centering[..., None])).astype(jnp.bfloat16)
    scaling = queries.shape[-1] ** (-0.5)
    query_grad = (
        jnp.einsum("kgij,jkd->ikgd", score_grad, key_block, preferred_element_type=jnp.float32)
        * scaling
    )
    key_grad = (
        jnp.einsum("kgij,ikgd->jkd", score_grad, queries, preferred_element_type=jnp.float32)
        * scaling
    )
    return (query_grad, key_grad, value_grad)


def per_device(
    delta_query,
    delta_key,
    delta_value,
    beta_logit,
    decay_input,
    decay_log,
    norm_gain,
    output_gate,
    delta_cotangent,
    attn_query,
    attn_key,
    attn_value,
    attn_gate,
    attn_cotangent,
):
    tokens = delta_query.shape[1]
    heads_here = decay_log.shape[0]
    head_size = norm_gain.shape[0]
    flat = (1, tokens, heads_here * head_size)

    def by_heads(array):
        return array[0].astype(jnp.float32).reshape(tokens, heads_here, head_size)

    queries = by_heads(delta_query)
    keys_in = by_heads(delta_key)
    values = by_heads(delta_value)
    gate_values = by_heads(output_gate)
    beta_in = beta_logit[0]
    decay_in = decay_input[0]
    unit_queries, unit_keys, beta_values, decays = delta_inputs(
        queries, keys_in, beta_in, decay_in, decay_log
    )
    identity = jnp.broadcast_to(
        jnp.eye(head_size, dtype=jnp.float32), (heads_here, head_size, head_size)
    )
    blank_state = jnp.zeros((heads_here, head_size, head_size), jnp.float32)

    def fold_block(carried, pieces):
        return (compose(carried, block_map(*pieces)), None)

    block_pieces = (
        split_rows(unit_keys, BLOCK_LEN),
        split_rows(values, BLOCK_LEN),
        split_rows(beta_values, BLOCK_LEN),
        split_rows(decays, BLOCK_LEN),
    )
    transfer, offset = lax.scan(fold_block, (identity, blank_state), block_pieces)[0]

    def relay_step(relay_turn, incoming):
        leaving = jnp.einsum("hij,hjk->hik", incoming, transfer, precision=HIGHEST) + offset
        return passed_along(leaving, "ctx", 1)

    state_in = lax.fori_loop(0, lax.axis_size("ctx") - 1, relay_step, blank_state)

    def layer_piece(
        state_start,
        queries_in,
        keys_part,
        values_in,
        beta_part,
        decay_part,
        decay_rates,
        gain_in,
        gates_in,
    ):
        return delta_layer(
            state_start,
            queries_in,
            keys_part,
            values_in,
            beta_part,
            decay_part,
            decay_rates,
            gain_in,
            gates_in,
            BLOCK_LEN,
        )

    (result, state_end), pullback = jax.vjp(
        layer_piece,
        state_in,
        queries,
        keys_in,
        values,
        beta_in,
        decay_in,
        decay_log,
        norm_gain,
        gate_values,
    )
    cotangent = by_heads(delta_cotangent)
    local_part = pullback((cotangent, jnp.zeros_like(state_end)))[0]
    state_grad = carried_in(
        (jnp.swapaxes(transfer, 1, 2), local_part), "ctx", compose, (identity, blank_state)
    )[1]
    gradients = pullback((cotangent, state_grad))
    decay_log_grad = lax.psum(gradients[6], ("ctx", "section"))
    gain_grad = lax.psum(gradients[7], ("ctx", "head", "section"))
    tokens_att = attn_query.shape[1]
    kv_here = attn_key.shape[2] // AD
    group_size = attn_query.shape[2] // (kv_here * AD)
    shape_four = (tokens_att, kv_here, group_size, AD)
    query_att = attn_query[0].reshape(shape_four)
    keys_all, values_all = (
        lax.all_gather(attn_key, "ctx", axis=1, tiled=True),
        lax.all_gather(attn_value, "ctx", axis=1, tiled=True),
    )
    length = keys_all.shape[1]
    keys_all = keys_all[0].reshape(length, kv_here, AD)
    values_all = values_all[0].reshape(length, kv_here, AD)
    query_start = lax.axis_index("ctx") * tokens_att
    attended, log_total = attend(query_att, keys_all, values_all, query_start)
    opening = jax.nn.sigmoid(attn_gate[0].reshape(shape_four).astype(jnp.float32))
    cotangent_att = attn_cotangent[0].reshape(shape_four).astype(jnp.float32)
    attn_out = (attended * opening).astype(jnp.bfloat16)
    upstream = (cotangent_att * opening).astype(jnp.bfloat16)
    gate_grad = (cotangent_att * attended * opening * (1.0 - opening)).astype(jnp.bfloat16)
    centering = jnp.transpose(jnp.sum(upstream.astype(jnp.float32) * attended, axis=-1), (1, 2, 0))
    key_blocks, value_blocks, starts = key_blocks_of(keys_all, values_all)
    width_kv = kv_here * AD

    def whole_step(running, pieces):
        key_block, value_block, key_start = pieces
        query_grad, key_grad, value_grad = key_block_grads(
            query_att,
            key_block,
            value_block,
            query_start,
            key_start,
            log_total,
            upstream,
            centering,
        )
        rows_here = key_block.shape[0]
        return (
            running + query_grad,
            jnp.concatenate(
                [key_grad.reshape(rows_here, width_kv), value_grad.reshape(rows_here, width_kv)],
                axis=-1,
            ),
        )

    query_total, key_terms = lax.scan(
        whole_step, jnp.zeros(shape_four, jnp.float32), (key_blocks, value_blocks, starts)
    )
    own_rows = lax.psum_scatter(
        key_terms.reshape(length, 2 * width_kv), "ctx", scatter_dimension=0, tiled=True
    )
    attn_flat = (1, tokens_att, kv_here * group_size * AD)
    return (
        result.reshape(flat).astype(jnp.bfloat16),
        gradients[1].reshape(flat).astype(jnp.bfloat16),
        gradients[2].reshape(flat).astype(jnp.bfloat16),
        gradients[3].reshape(flat).astype(jnp.bfloat16),
        gradients[4][None],
        gradients[5][None],
        decay_log_grad,
        gain_grad,
        gradients[8].reshape(flat).astype(jnp.bfloat16),
        attn_out.reshape(attn_flat),
        query_total.reshape(attn_flat).astype(jnp.bfloat16),
        own_rows[:, :width_kv].astype(jnp.bfloat16)[None],
        own_rows[:, width_kv:].astype(jnp.bfloat16)[None],
        gate_grad.reshape(attn_flat),
    )


def solution(mesh):
    in_specs = (
        P("section", "ctx", "head"),
        P("section", "ctx", "head"),
        P("section", "ctx", "head"),
        P("section", "ctx", "head"),
        P("section", "ctx", "head"),
        P("head"),
        P(),
        P("section", "ctx", "head"),
        P("section", "ctx", "head"),
        P("section", "ctx", "head"),
        P("section", "ctx", "head"),
        P("section", "ctx", "head"),
        P("section", "ctx", "head"),
        P("section", "ctx", "head"),
    )
    out_specs = (
        P("section", "ctx", "head"),
        P("section", "ctx", "head"),
        P("section", "ctx", "head"),
        P("section", "ctx", "head"),
        P("section", "ctx", "head"),
        P("section", "ctx", "head"),
        P("head"),
        P(),
        P("section", "ctx", "head"),
        P("section", "ctx", "head"),
        P("section", "ctx", "head"),
        P("section", "ctx", "head"),
        P("section", "ctx", "head"),
        P("section", "ctx", "head"),
    )
    return jax.shard_map(
        per_device, mesh=mesh, in_specs=in_specs, out_specs=out_specs, check_vma=False
    )
```

profile of v0, /device:TPU:0, one launch (start us, length us, event | category | flops | bytes accessed | tf_op | source)
XLA Modules:
  0.0 1342.6 jit_solution(9925654964251903337)
XLA Ops:
  13.2 43.6 %all-gather.9.cloned.1.call-done = bf16[1,4096,256]{2,1,0:T(8,128)(2,1)} async-done(((bf16[1,128,256]{2,1,0:T(8,128)(2,1)}), bf16[1,4096,256]{2,1,0:T(8,128)(2,1)}) %all-gather.9.cloned.1.call-update) | async-done | bytes 2097168 | tf_op jit(solution)/shard_map/all_gather | solution.py:350
  56.8 26.8 %while.216 = (s32[]{:T(128)}, f32[1,8,128]{2,1,0:T(8,128)S(1)}, f32[1,8,128]{2,1,0:T(8,128)S(1)}, s32[8]{0:T(128)S(1)}, s32[]{:T(128)}, /*index=5*/bf16[8,512,1,...) while((s32[]{:T(128)}, f32[1,8,128]{2,1,0:T(8,128)S(1)}, ...), condition=%wide.region_37.38_spmd.clone, body=%wide.region_34.37_spmd.clone.sunk | while | flops 272176768 | bytes 5235848 | solution.py:201
  83.6 18.7 %all-gather.7.cloned.1.call-done = bf16[1,4096,256]{2,1,0:T(8,128)(2,1)} async-done(((bf16[1,128,256]{2,1,0:T(8,128)(2,1)}), bf16[1,4096,256]{2,1,0:T(8,128)(2,1)}) %all-gather.7.cloned.1.call-update) | async-done | bytes 2097168 | tf_op jit(solution)/shard_map/all_gather | solution.py:351
  102.3 36.9 %while.217 = (s32[]{:T(128)}, f32[128,1,8,256]{0,3,2,1:T(8,128)}, bf16[8,512,1,256]{3,1,2,0:T(8,128)(2,1)}, s32[8]{0:T(128)S(1)}, s32[]{:T(128)}, /*index=5*/bf1...) while((s32[]{:T(128)}, f32[128,1,8,256]{0,3,2,1:T(8,128)}, ...), condition=%wide.region_39.40_spmd.clone, body=%wide.region_38.39_spmd.clone.sunk | while | flops 539558528 | bytes 3287690 | solution.py:216
  141.9 84.8 %while.218 = (s32[]{:T(128)}, f32[128,1,8,256]{0,3,2,1:T(8,128)}, f32[8,512,512]{2,1,0:T(8,128)}, bf16[8,512,1,256]{3,1,2,0:T(8,128)(2,1)}, s32[8]{0:T(128)S(1)}...) while((s32[]{:T(128)}, f32[128,1,8,256]{0,3,2,1:T(8,128)}, ...), condition=%wide.region_42.43_spmd.clone, body=%wide.region_41.42_spmd.clone.sunk | while | flops 1347093120 | bytes 30291236 | solution.py:388
  229.7 20.7 %while.213 = (s32[]{:T(128)}, f32[8,128,128]{1,2,0:T(8,128)S(1)}, f32[8,128,128]{1,2,0:T(8,128)S(1)}, f32[2,8,64]{2,1,0:T(8,128)S(1)}, f32[2,8,64]{2,1,0:T(8,128...) while((s32[]{:T(128)}, f32[8,128,128]{1,2,0:T(8,128)S(1)}, ...), condition=%wide.region_3.4_spmd.clone, body=%wide.region_1.3_spmd.clone.sunk | while | flops 1007862272 | bytes 12360503 | solution.py:292
  259.9 469.8 %while.210 = (s32[]{:T(128)}, f32[8,128,128]{2,1,0:T(8,128)S(1)}, f32[8,128,128]{2,1,0:T(8,128)}, f32[8,128,128]{2,1,0:T(8,128)}, s32[]{:T(128)}) while((s32[]{:T(128)}, f32[8,128,128]{2,1,0:T(8,128)S(1)}, f32[8,128,128]{2,1,0:T(8,128)}, f32[8,128,128]{2,1,0:T(8,128)}, s32[]{:T(128)}) %tuple.379), condition=%wide.region_5.6_spmd, body=%wide.region_4.5_spmd.sunk | while | flops 201457664 | bytes 4194405 | solution.py:298
  281.6 20.2 %collective-permute-start = (f32[8,128,128]{2,1,0:T(8,128)}, f32[8,128,128]{2,1,0:T(8,128)S(1)}, u32[]{:S(2)}, u32[]{:S(2)}) collective-permute-start(f32[8,128,128]{2,1,0:T(8,128)} %convolution_add_fusion.46), channel_id=1, source_target_pairs={{0,4},{4,8},{8,12},{12,16},{16,20},{20,24},{24,28},{28,32},{32,36}... | collective-permute-start | bytes 1572872 | tf_op jit(solution)/shard_map/while/body/eval_jaxpr/ppermute | solution.py:17
  334.3 12.2 collective-permute-start
  365.4 19.5 %collective-permute-start = (f32[8,128,128]{2,1,0:T(8,128)}, f32[8,128,128]{2,1,0:T(8,128)S(1)}, u32[]{:S(2)}, u32[]{:S(2)}) collective-permute-start(f32[8,128,128]{2,1,0:T(8,128)} %convolution_add_fusion.46), channel_id=1, source_target_pairs={{0,4},{4,8},{8,12},{12,16},{16,20},{20,24},{24,28},{28,32},{32,36}... | collective-permute-start | bytes 1572872 | tf_op jit(solution)/shard_map/while/body/eval_jaxpr/ppermute | solution.py:17
  389.3 19.4 %collective-permute-start = (f32[8,128,128]{2,1,0:T(8,128)}, f32[8,128,128]{2,1,0:T(8,128)S(1)}, u32[]{:S(2)}, u32[]{:S(2)}) collective-permute-start(f32[8,128,128]{2,1,0:T(8,128)} %convolution_add_fusion.46), channel_id=1, source_target_pairs={{0,4},{4,8},{8,12},{12,16},{16,20},{20,24},{24,28},{28,32},{32,36}... | collective-permute-start | bytes 1572872 | tf_op jit(solution)/shard_map/while/body/eval_jaxpr/ppermute | solution.py:17
  546.9 11.1 collective-permute-start
  577.8 11.1 collective-permute-start
  593.2 11.1 collective-permute-start
  608.7 11.1 collective-permute-start
  624.2 11.1 collective-permute-start
  655.1 11.1 collective-permute-start
  686.0 11.1 collective-permute-start
  716.9 11.1 collective-permute-start
  735.7 45.5 %while.211 = (s32[]{:T(128)}, f32[8,128,128]{2,1,0:T(8,128)S(1)}, f32[2,8,64,128]{3,2,1,0:T(8,128)}, f32[2,8,64,64]{3,2,1,0:T(8,128)S(1)}, f32[2,8,64,1]{2,1,3,0...) while((s32[]{:T(128)}, f32[8,128,128]{2,1,0:T(8,128)S(1)}, ...), condition=%wide.region_9.10_spmd.clone.clone, body=%wide.region_7.9_spmd.clone.clone.sunk | while | flops 807413760 | bytes 76981544 | solution.py:159
  803.3 115.1 %psum.15 = f32[128]{0:T(128)} all-reduce(f32[128]{0:T(128)S(1)} %get-tuple-element.3540), channel_id=1, replica_groups=mesh['ctx'=32,'head'=2,'section'=2] {'ctx','head','section'}, use_global_device_ids=true, to_apply=%region_33.34 | all-reduce | flops 128 | bytes 1024 | tf_op jit(solution)/shard_map/psum | solution.py:343
  929.6 165.9 %while.215 = (s32[]{:T(128)}, f32[8,128,128]{1,2,0:T(8,128)}, s32[]{:T(128)}, f32[32,8,128,128]{3,2,1,0:T(8,128)}, f32[32,8,128,128]{3,2,1,0:T(8,128)}, /*index=5*/s32[]{:T(128)}, s32[]{:T(128)}, s32[]{:T(128)}, s32[]{:T(128)}) while((s32[]{:T(128)}, f32[8,128,128]{1,2,0:T(8,128)}, s32[]{:T(128)}, ...), condition=%wide.region_15.16_spmd.clone, body=%wide.region_14.15_spmd.clone.sunk | while | flops 201850880 | bytes 5769385 | solution.py:35
  1098.5 59.1 %while.212 = (s32[]{:T(128)}, f32[8,128,128]{2,1,0:T(8,128)S(1)}, f32[2,8,64,128]{3,1,2,0:T(8,128)}, f32[2,8,64,128]{3,2,1,0:T(8,128)}, bf16[2,8,64,128]{3,2,1,0...) while((s32[]{:T(128)}, f32[8,128,128]{2,1,0:T(8,128)S(1)}, ...), condition=%wide.region_27.28_spmd.clone.clone, body=%wide.region_16.27_spmd.clone.clone.sunk | while | flops 1613599232 | bytes 80876960 | solution.py:159
  1166.8 166.0 %psum.14 = f32[8]{0:T(128)} all-reduce(f32[8]{0:T(128)S(1)} %negate_multiply_fusion), channel_id=1, replica_groups=mesh['ctx'=32,'head'=2,'section'=2] {'ctx','section'}, use_global_device_ids=true, to_apply=%region_31.32 | all-reduce | flops 8 | bytes 64 | tf_op jit(solution)/shard_map/psum | solution.py:342
  (1251 shorter events, 828.2 us)
Async XLA Ops:
  7.2 49.6 %all-gather.9.cloned.1.call-start = ((), (), s32[]{:S(2)}) async-start(), calls=%async_computation.2 | async-start | bytes 2162688 | tf_op jit(solution)/shard_map/all_gather | solution.py:350
  7.9 94.4 %all-gather.7.cloned.1.call-start = ((), (), s32[]{:S(2)}) async-start(), calls=%async_computation.1 | async-start | bytes 2162688 | tf_op jit(solution)/shard_map/all_gather | solution.py:351
  8.7 919.3 %reduce-scatter.2.cloned.1.call-start = ((), (), s32[]{:S(2)}) async-start(), calls=%async_computation.3 | async-start | bytes 8650752 | tf_op jit(solution)/shard_map/reduce_scatter | solution.py:391
  226.7 702.9 %all-gather.11.cloned.1.call-start = ((), (), s32[]{:S(2)}) async-start(), calls=%async_computation.4 | async-start | bytes 17301504 | tf_op jit(solution)/shard_map/all_gather | solution.py:22
  251.2 678.4 %all-gather.13.cloned.1.call-start = ((), (), s32[]{:S(2)}) async-start(), calls=%async_computation.5 | async-start | bytes 17301504 | tf_op jit(solution)/shard_map/all_gather | solution.py:22
  281.6 21.9 %collective-permute-start = (f32[8,128,128]{2,1,0:T(8,128)}, f32[8,128,128]{2,1,0:T(8,128)S(1)}, u32[]{:S(2)}, u32[]{:S(2)}) collective-permute-start(f32[8,128,128]{2,1,0:T(8,128)} %convolution_add_fusion.46), channel_id=1, source_target_pairs={{0,4},{4,8},{8,12},{12,16},{16,20},{20,24},{24,28},{28,32},{32,36}... | collective-permute-start | bytes 1572872 | tf_op jit(solution)/shard_map/while/body/eval_jaxpr/ppermute | solution.py:17
  319.6 12.1 collective-permute-start
  334.3 13.9 %collective-permute-start = (f32[8,128,128]{2,1,0:T(8,128)}, f32[8,128,128]{2,1,0:T(8,128)S(1)}, u32[]{:S(2)}, u32[]{:S(2)}) collective-permute-start(f32[8,128,128]{2,1,0:T(8,128)} %convolution_add_fusion.46), channel_id=1, source_target_pairs={{0,4},{4,8},{8,12},{12,16},{16,20},{20,24},{24,28},{28,32},{32,36}... | collective-permute-start | bytes 1572872 | tf_op jit(solution)/shard_map/while/body/eval_jaxpr/ppermute | solution.py:17
  350.9 11.9 collective-permute-start
  365.4 21.2 %collective-permute-start = (f32[8,128,128]{2,1,0:T(8,128)}, f32[8,128,128]{2,1,0:T(8,128)S(1)}, u32[]{:S(2)}, u32[]{:S(2)}) collective-permute-start(f32[8,128,128]{2,1,0:T(8,128)} %convolution_add_fusion.46), channel_id=1, source_target_pairs={{0,4},{4,8},{8,12},{12,16},{16,20},{20,24},{24,28},{28,32},{32,36}... | collective-permute-start | bytes 1572872 | tf_op jit(solution)/shard_map/while/body/eval_jaxpr/ppermute | solution.py:17
  389.3 21.2 %collective-permute-start = (f32[8,128,128]{2,1,0:T(8,128)}, f32[8,128,128]{2,1,0:T(8,128)S(1)}, u32[]{:S(2)}, u32[]{:S(2)}) collective-permute-start(f32[8,128,128]{2,1,0:T(8,128)} %convolution_add_fusion.46), channel_id=1, source_target_pairs={{0,4},{4,8},{8,12},{12,16},{16,20},{20,24},{24,28},{28,32},{32,36}... | collective-permute-start | bytes 1572872 | tf_op jit(solution)/shard_map/while/body/eval_jaxpr/ppermute | solution.py:17
  533.3 11.0 collective-permute-start
  546.9 12.8 collective-permute-start
  562.3 12.8 collective-permute-start
  577.8 12.8 collective-permute-start
  593.2 12.8 collective-permute-start
  608.7 12.8 collective-permute-start
  624.2 12.8 collective-permute-start
  639.6 12.8 collective-permute-start
  655.1 12.8 collective-permute-start
  670.5 12.8 collective-permute-start
  686.0 12.8 collective-permute-start
  701.4 12.8 collective-permute-start
  716.9 12.8 collective-permute-start
  (228 other events, 1415.9 us)
Sparse Core Ops, SparseCore 0:
  10.3 46.4 all-gather.8
  59.1 43.2 all-gather.6
  226.8 97.9 reduce-scatter.1
  327.2 81.5 all-gather.10
  796.9 121.4 all-gather.12
where the time goes:
time: 1360 us; the launch traced here: 1340 us
  matrix products  376 us (28%)
  starting transfers between devices  334 us (25%)
  blocking collectives  281 us (21%)
  local copies, waits for them, and re-layouts  163 us (12%)
  waiting for transfers between devices  117 us (9%)
  other arithmetic  50.2 us (4%)
  between operations  15.2 us (1%)
    ppermute x31, starting transfers between devices, passed_along(): return lax.ppermute(block, axis, route)  334 us
    psum x1, blocking collectives, per_device(): decay_log_grad = lax.psum(gradients[6], ('ctx', 'section'))  166 us
    psum x1, blocking collectives, per_device(): gain_grad = lax.psum(gradients[7], ('ctx', 'head', 'section'))  115 us
    dot_general x34, matrix products, compose(): jnp.einsum('hij,hjk->hik', earlier[1], later[0], precision=HIGHEST)  93.4 us
    dot_general x31, matrix products, relay_step(): jnp.einsum('hij,hjk->hik', incoming, transfer, precision=HIGHEST) + offset  82.2 us
    ppermute x31, waiting for transfers between devices, passed_along(): return lax.ppermute(block, axis, route)  53.2 us
    all_gather x1, waiting for transfers between devices, per_device(): lax.all_gather(attn_key, 'ctx', axis=1, tiled=True)  43.6 us
    dynamic_slice x64, local copies, waits for them, and re-layouts, lap(): new = combine(before, jax.tree.map(lambda part: part[at], everything))  40.7 us
  transfers between devices with their start and end apart: 36, of which 33 were waited for; matrix products, arithmetic and copies ran while one was open for 16% of the time, Pallas kernels for 0%

commit v1 on v0

v1 whole, which is shorter than its diff:
```python
import functools

import jax
import jax.numpy as jnp
from jax import lax
from jax.experimental import pallas as pl
from jax.experimental.pallas import tpu as pltpu
from jax.sharding import PartitionSpec as P

f32, bf16 = jnp.float32, jnp.bfloat16
MESH = pl.DeviceIdType.MESH
HIGHEST = lax.Precision.HIGHEST
NEG_FILL = -1e30
N = 32
C = 128
DK = 128
AD = 256
HEADS = 8
GROUP = 8
ROWS = GROUP * C
KB = 512
LENGTH = N * C
NKB = LENGTH // KB
QUARTERS = N // HEADS
SROWS = DK // QUARTERS
VMEM_BIG = 60 * 1024 * 1024

NT = (((1,), (1,)), ((), ()))
NN = (((1,), (0,)), ((), ()))
TN = (((0,), (0,)), ((), ()))


def d1(a, b, dims):
    return lax.dot_general(a.astype(bf16), b.astype(bf16), dims, preferred_element_type=f32)


def split(a):
    hi = a.astype(bf16)
    return hi, (a - hi.astype(f32)).astype(bf16)


def d3(a, b, dims):
    ah, al = split(a)
    bh, bl = split(b)

    def dot(x, y):
        return lax.dot_general(x, y, dims, preferred_element_type=f32)

    return dot(ah, bh) + (dot(ah, bl) + dot(al, bh))


def dfull(a, b, dims):
    return lax.dot_general(a, b, dims, precision=HIGHEST, preferred_element_type=f32)


def iotas(shape=(C, C)):
    return (
        lax.broadcasted_iota(jnp.int32, shape, 0),
        lax.broadcasted_iota(jnp.int32, shape, 1),
    )


def unit(x):
    r = lax.rsqrt(jnp.sum(x * x, axis=-1, keepdims=True) + 1e-6)
    return x * r, r


def gates_of(bl_ref, di_ref, dl_ref):
    beta = 1.0 / (1.0 + jnp.exp(-bl_ref[...]))
    a = di_ref[...]
    rate = -jnp.exp(dl_ref[...])
    soft = jnp.maximum(a, 0.0) + jnp.log1p(jnp.exp(-jnp.abs(a)))
    g = jnp.maximum(rate * soft, -104.0)
    r, c = iotas()
    beta_cols = dfull(jnp.where(r == c, 1.0, 0.0), beta, NT)
    cols = dfull(jnp.where(r >= c, 1.0, 0.0), g, NT)
    rows = dfull(g, jnp.where(r <= c, 1.0, 0.0), NN)
    return beta, g, rate, beta_cols, cols, rows


def fade(cc, cr):
    r, c = iotas()
    return jnp.where(r >= c, jnp.exp(jnp.where(r >= c, cc - cr, 0.0)), 0.0)


def head_cols(ref, h):
    return ref[:, h * DK : (h + 1) * DK].astype(f32)


def chunk_kernel(k_ref, v_ref, bl_ref, di_ref, dl_ref, n_ref, w_ref, u0_ref, m_ref, o_ref):
    _, _, _, beta, cols, rows = gates_of(bl_ref, di_ref, dl_ref)
    r, c = iotas()
    group = 4

    for first in range(0, HEADS, group):
        heads = range(first, first + group)
        ks = [unit(head_cols(k_ref, h))[0] for h in heads]
        low = []
        for h, K in zip(heads, ks):
            F = fade(cols[:, h : h + 1], rows[h : h + 1, :])
            low.append(jnp.where(r > c, beta[:, h : h + 1] * F * d1(K, K, NT), 0.0))
        inv = [
            jnp.where(r == c, 1.0, 0.0) - jnp.where(r // 2 == c // 2, L, 0.0) for L in low
        ]
        k = 2
        while k < C:
            part = (r // (2 * k) == c // (2 * k)) & (r // k != c // k)
            mid = [d1(I, jnp.where(part, L, 0.0), NN) for I, L in zip(inv, low)]
            inv = [I - d1(T, I, NN) for I, T in zip(inv, mid)]
            k *= 2
        for h, K, I in zip(heads, ks, inv):
            b, cc = beta[:, h : h + 1], cols[:, h : h + 1]
            V = head_cols(v_ref, h)
            W = d3(I, (b * jnp.exp(cc)) * K, NN)
            U0 = d3(I, b * V, NN)
            cl = cc[C - 1 : C, :]
            Kt = jnp.exp(cl - cc) * K
            n_ref[h] = I
            w_ref[h] = W
            u0_ref[h] = U0
            m_ref[h] = (-d3(W, Kt, TN)).astype(bf16)
            off = d3(U0, Kt, TN)
            keep = jnp.broadcast_to(jnp.exp(cl), (8, DK))
            for q in range(QUARTERS):
                o_ref[h * QUARTERS + q, 0:SROWS, :] = off[q * SROWS : (q + 1) * SROWS, :]
                o_ref[h * QUARTERS + q, SROWS : SROWS + 8, :] = keep


def greet(me):
    barrier = pltpu.get_barrier_semaphore()

    def hello(p, carry):
        pl.semaphore_signal(
            barrier, inc=1, device_id={"ctx": lax.rem(me + p, N)}, device_id_type=MESH
        )
        return carry

    lax.fori_loop(1, N, hello, 0)
    pl.semaphore_wait(barrier, N - 1)


def remote(src, dst, send, recv, peer):
    return pltpu.make_async_remote_copy(
        src_ref=src,
        dst_ref=dst,
        send_sem=send,
        recv_sem=recv,
        device_id={"ctx": peer},
        device_id_type=MESH,
    )


def advanced(S, M, dims):
    hi, lo = split(S)
    both = jnp.concatenate([hi.astype(f32), lo.astype(f32)], axis=0).astype(bf16)
    out = lax.dot_general(both, M, dims, preferred_element_type=f32)
    return out[:SROWS] + out[SROWS:]


def forward_exchange(
    m_ref, o_ref, mall, eall, srecv, oall, sbuf, m_send, m_recv, o_send, o_recv, s_send, s_recv
):
    me = lax.axis_index("ctx")
    greet(me)

    def send(p, carry):
        peer = lax.rem(me + p, N)
        remote(m_ref.at[peer // QUARTERS], mall.at[me], m_send.at[p], m_recv.at[me], peer).start()
        remote(o_ref.at[peer], oall.at[me], o_send.at[p], o_recv.at[me], peer).start()
        return carry

    lax.fori_loop(1, N, send, 0)
    mall[me] = m_ref[me // QUARTERS]
    oall[me] = o_ref[me]

    def step(s, S):
        @pl.when(s != me)
        def _():
            remote(m_ref.at[0], mall.at[s], m_send.at[0], m_recv.at[s], s).wait_recv()
            remote(o_ref.at[0], oall.at[s], o_send.at[0], o_recv.at[s], s).wait_recv()

        sbuf[s] = S

        @pl.when(s != me)
        def _():
            remote(sbuf.at[s], srecv.at[me], s_send.at[s], s_recv.at[me], s).start()

        keep = oall[s, SROWS : SROWS + 8, :]
        eall[s] = keep
        return keep[0:1, :] * S + advanced(S, mall[s], NN) + oall[s, 0:SROWS, :]

    lax.fori_loop(0, N, step, jnp.zeros((SROWS, DK), f32))
    srecv[me] = sbuf[me]

    def finish(p, carry):
        peer = lax.rem(me + p, N)
        remote(m_ref.at[0], mall.at[me], m_send.at[p], m_recv.at[me], peer).wait_send()
        remote(o_ref.at[0], oall.at[me], o_send.at[p], o_recv.at[me], peer).wait_send()
        remote(sbuf.at[peer], srecv.at[me], s_send.at[peer], s_recv.at[me], peer).wait_send()
        remote(sbuf.at[peer], srecv.at[peer], s_send.at[peer], s_recv.at[peer], peer).wait_recv()
        return carry

    lax.fori_loop(1, N, finish, 0)


def backward_exchange(
    mall, eall, l_ref, srecv, lall, sbuf, l_send, l_recv, s_send, s_recv
):
    me = lax.axis_index("ctx")
    greet(me)

    def send(p, carry):
        peer = lax.rem(me + p, N)
        remote(l_ref.at[peer], lall.at[me], l_send.at[p], l_recv.at[me], peer).start()
        return carry

    lax.fori_loop(1, N, send, 0)
    lall[me] = l_ref[me]

    def step(k, S):
        s = N - 1 - k
        sbuf[s] = S

        @pl.when(s != me)
        def _():
            remote(sbuf.at[s], srecv.at[me], s_send.at[s], s_recv.at[me], s).start()
            remote(l_ref.at[0], lall.at[s], l_send.at[0], l_recv.at[s], s).wait_recv()

        return eall[s, 0:1, :] * S + advanced(S, mall[s], NT) + lall[s]

    lax.fori_loop(0, N, step, jnp.zeros((SROWS, DK), f32))
    srecv[me] = sbuf[me]

    def finish(p, carry):
        peer = lax.rem(me + p, N)
        remote(l_ref.at[0], lall.at[me], l_send.at[p], l_recv.at[me], peer).wait_send()
        remote(sbuf.at[peer], srecv.at[me], s_send.at[peer], s_recv.at[me], peer).wait_send()
        remote(sbuf.at[peer], srecv.at[peer], s_send.at[peer], s_recv.at[peer], peer).wait_recv()
        return carry

    lax.fori_loop(1, N, finish, 0)


def output_kernel(
    s_ref, q_ref, k_ref, w_ref, u0_ref, bl_ref, di_ref, dl_ref, gain_ref, gate_ref, cot_ref,
    out_ref, dgate_ref, dgain_ref, u_ref, do_ref, dul_ref, dsl_ref,
):
    _, _, _, _, cols, rows = gates_of(bl_ref, di_ref, dl_ref)
    gain = gain_ref[...]
    gain_sum = jnp.zeros((1, DK), f32)
    for h in range(HEADS):
        at = slice(h * DK, (h + 1) * DK)
        Q = unit(head_cols(q_ref, h))[0] * DK**-0.5
        K = unit(head_cols(k_ref, h))[0]
        S, W = s_ref[h], w_ref[h]
        cc = cols[:, h : h + 1]
        ec = jnp.exp(cc)
        F = fade(cc, rows[h : h + 1, :])
        U = u0_ref[h] - d3(W, S, NT)
        Pm = d3(Q, K, NT) * F
        m = ec * d3(Q, S, NT) + d3(Pm, U, NN)
        rr = lax.rsqrt(jnp.mean(m * m, axis=-1, keepdims=True) + 1e-6)
        gate = head_cols(gate_ref, h)
        cot = head_cols(cot_ref, h)
        sig = 1.0 / (1.0 + jnp.exp(-gate))
        silu = gate * sig
        nm = m * rr
        out_ref[:, at] = (nm * gain * silu).astype(bf16)
        dgate_ref[:, at] = (cot * nm * gain * (sig * (1.0 + gate * (1.0 - sig)))).astype(bf16)
        gain_sum = gain_sum + jnp.sum(cot * nm * silu, axis=0, keepdims=True)
        dn = cot * gain * silu
        dO = rr * dn - m * (rr * rr * rr) * jnp.mean(m * dn, axis=-1, keepdims=True)
        dUl = d3(Pm, dO, TN)
        u_ref[h] = U
        do_ref[h] = dO
        dul_ref[h] = dUl
        dsl_ref[h] = d3(ec * dO, Q, TN) - d3(dUl, W, TN)
    dgain_ref[...] = gain_sum


def gradient_kernel(
    s_ref, ds_ref, q_ref, k_ref, v_ref, n_ref, u_ref, do_ref, dul_ref, bl_ref, di_ref, dl_ref,
    dgain_ref, dq_ref, dk_ref, dv_ref, dbl_ref, ddi_ref, sums_ref,
):
    beta_rows, g, rate, beta, cols, rows = gates_of(bl_ref, di_ref, dl_ref)
    r, c = iotas()
    lane = lax.broadcasted_iota(jnp.int32, (C, DK), 1)
    sub = lax.broadcasted_iota(jnp.int32, (HEADS, C), 0)
    dbeta = jnp.zeros((C, DK), f32)
    dcol = jnp.zeros((C, DK), f32)
    drow = jnp.zeros((HEADS, C), f32)
    dlast = jnp.zeros((HEADS, C), f32)
    for h in range(HEADS):
        at = slice(h * DK, (h + 1) * DK)
        xq, xk = head_cols(q_ref, h), head_cols(k_ref, h)
        Q0, rq = unit(xq)
        Q = Q0 * DK**-0.5
        K, rk = unit(xk)
        V = head_cols(v_ref, h)
        S, dS, I, U, dO, dUl = s_ref[h], ds_ref[h], n_ref[h], u_ref[h], do_ref[h], dul_ref[h]
        b, cc = beta[:, h : h + 1], cols[:, h : h + 1]
        ec = jnp.exp(cc)
        F = fade(cc, rows[h : h + 1, :])
        cl = cc[C - 1 : C, :]
        tail = jnp.exp(cl - cc)
        A = d1(K, K, NT)
        QK = d3(Q, K, NT)
        dU = dUl + d3(tail * K, dS, NT)
        QS = ec * d3(Q, S, NT)
        Y = d3(K, S, NT)
        dPF = d3(dO, U, NT) * F
        dQ = ec * d3(dO, S, NN) + d3(dPF, K, NN)
        dKt = tail * d3(U, dS, NN)
        tau = jnp.sum(dKt * K, axis=-1, keepdims=True)
        dcl = jnp.sum(tau, axis=0, keepdims=True) + jnp.exp(cl) * jnp.sum(
            jnp.sum(dS * S, axis=-1, keepdims=True), axis=0, keepdims=True
        )
        dR = d3(I, dU, TN)
        dV = b * dR
        dY = (-ec) * dV
        dLF = jnp.where(r > c, -d3(dR, U, NT), 0.0) * F
        G2 = dLF * A
        db = jnp.sum(dR * (V - ec * Y), axis=-1, keepdims=True) + jnp.sum(
            G2, axis=-1, keepdims=True
        )
        dA = b * dLF
        dK = d3(dPF, Q, TN) + dKt + d3(dY, S, NN) + d3(dA, K, NN) + d3(dA, K, TN)
        G = dPF * QK + b * G2
        dcc = jnp.sum(dO * QS + dY * Y, axis=-1, keepdims=True) - tau + jnp.sum(
            G, axis=-1, keepdims=True
        )
        dbeta = jnp.where(lane == h, db, dbeta)
        dcol = jnp.where(lane == h, dcc, dcol)
        drow = jnp.where(sub == h, -jnp.sum(G, axis=0, keepdims=True), drow)
        dlast = jnp.where(sub == h, dcl, dlast)
        dq_ref[:, at] = (
            DK**-0.5 * (rq * dQ - xq * (rq * rq * rq) * jnp.sum(xq * dQ, axis=-1, keepdims=True))
        ).astype(bf16)
        dk_ref[:, at] = (
            rk * dK - xk * (rk * rk * rk) * jnp.sum(xk * dK, axis=-1, keepdims=True)
        ).astype(bf16)
        dv_ref[:, at] = dV.astype(bf16)
    later = jnp.where(r >= c, 1.0, 0.0)
    dg = dfull(dcol, later, TN)[:HEADS] + dfull(drow, later, NN) + dlast
    dbeta = dfull(dbeta, jnp.where(r == c, 1.0, 0.0), TN)[:HEADS]
    dbl_ref[...] = dbeta * beta_rows * (1.0 - beta_rows)
    ddi_ref[...] = dg * rate / (1.0 + jnp.exp(-di_ref[...]))
    per_head = jnp.sum(dg * g, axis=1, keepdims=True)
    sums_ref[0:HEADS, :] = jnp.broadcast_to(per_head, (HEADS, DK))
    sums_ref[HEADS : 2 * HEADS, :] = jnp.broadcast_to(dgain_ref[...], (HEADS, DK))


def sum_kernel(x_ref, out_ref, every, part, others, send1, recv1, send2, recv2):
    me, head, section = (lax.axis_index(a) for a in ("ctx", "head", "section"))
    barrier = pltpu.get_barrier_semaphore()

    def hello(p, carry):
        pl.semaphore_signal(
            barrier, inc=1, device_id={"ctx": lax.rem(me + p, N)}, device_id_type=MESH
        )
        return carry

    lax.fori_loop(1, N, hello, 0)
    turns = ((0, 1), (1, 0), (1, 1))

    def aside(dh, ds):
        return {"head": lax.rem(head + dh, 2), "section": lax.rem(section + ds, 2)}

    for dh, ds in turns:
        pl.semaphore_signal(barrier, inc=1, device_id=aside(dh, ds), device_id_type=MESH)
    pl.semaphore_wait(barrier, N + 2)

    def send(p, carry):
        peer = lax.rem(me + p, N)
        remote(x_ref, every.at[me], send1.at[p], recv1.at[me], peer).start()
        return carry

    lax.fori_loop(1, N, send, 0)
    every[me] = x_ref[...]

    def finish(p, carry):
        peer = lax.rem(me + p, N)
        remote(x_ref, every.at[me], send1.at[p], recv1.at[me], peer).wait_send()
        remote(x_ref, every.at[peer], send1.at[p], recv1.at[peer], peer).wait_recv()
        return carry

    lax.fori_loop(1, N, finish, 0)
    part[...] = jnp.sum(every[...], axis=0)
    copies = [
        pltpu.make_async_remote_copy(
            src_ref=part,
            dst_ref=others.at[i],
            send_sem=send2.at[i],
            recv_sem=recv2.at[i],
            device_id=aside(dh, ds),
            device_id_type=MESH,
        )
        for i, (dh, ds) in enumerate(turns)
    ]
    for copy in copies:
        copy.start()
    for copy in copies:
        copy.wait()
    same = slice(0, HEADS)
    gain = slice(HEADS, 2 * HEADS)
    out_ref[same, :] = part[same, :] + others[0, same, :]
    out_ref[gain, :] = (part[gain, :] + others[0, gain, :]) + (
        others[1, gain, :] + others[2, gain, :]
    )


def attention_kernel(
    q_ref, gate_ref, cot_ref, kv_ref,
    out_ref, dq_ref, dgate_ref, dkv_ref,
    qs, ups, probs, att, dqt, top, low, cent,
):
    me = lax.axis_index("ctx")
    blocks = me // (KB // C) + 1
    scale = AD**-0.5
    width = 256
    parts = ROWS // width
    for g in range(GROUP):
        qs[g * C : (g + 1) * C, :] = (
            q_ref[:, g * AD : (g + 1) * AD].astype(f32) * scale
        ).astype(bf16)
    top[...] = jnp.full((8, ROWS), NEG_FILL, f32)
    low[...] = jnp.zeros((8, ROWS), f32)
    att[...] = jnp.zeros((AD, ROWS), f32)
    dqt[...] = jnp.zeros((AD, ROWS), f32)
    key_at, query_at = iotas((KB, width))
    reach = me * C + lax.rem(query_at, C) - key_at

    def rows_of(kb):
        return pl.ds(pl.multiple_of(kb * KB, KB), KB)

    def score(kb, carry):
        keys = kv_ref[rows_of(kb), 0:AD]
        for i in range(parts):
            cols = slice(i * width, (i + 1) * width)
            s = lax.dot_general(keys, qs[cols, :], NT, preferred_element_type=f32)
            s = jnp.where(reach >= kb * KB, s, NEG_FILL)
            probs[rows_of(kb), cols] = s
            top[:, cols] = jnp.maximum(
                top[:, cols], jnp.max(s.reshape(KB // 8, 8, width), axis=0)
            )
        return carry

    lax.fori_loop(0, blocks, score, 0)
    peak = jnp.max(top[...], axis=0, keepdims=True)
    top[...] = jnp.broadcast_to(peak, (8, ROWS))

    def weigh(kb, carry):
        values = kv_ref[rows_of(kb), AD : 2 * AD]
        for i in range(parts):
            cols = slice(i * width, (i + 1) * width)
            p = jnp.exp(probs[rows_of(kb), cols] - top[0:1, cols])
            probs[rows_of(kb), cols] = p
            low[:, cols] = low[:, cols] + jnp.sum(p.reshape(KB // 8, 8, width), axis=0)
            att[:, cols] = att[:, cols] + lax.dot_general(
                values, p.astype(bf16), TN, preferred_element_type=f32
            )
        return carry

    lax.fori_loop(0, blocks, weigh, 0)
    share = 1.0 / jnp.sum(low[...], axis=0, keepdims=True)
    low[...] = jnp.broadcast_to(share, (8, ROWS))
    for g in range(GROUP):
        cols = slice(g * C, (g + 1) * C)
        at = slice(g * AD, (g + 1) * AD)
        attended = jnp.transpose(att[:, cols] * low[0:1, cols])
        opening = 1.0 / (1.0 + jnp.exp(-gate_ref[:, at].astype(f32)))
        cot = cot_ref[:, at].astype(f32)
        out_ref[:, at] = (attended * opening).astype(bf16)
        up = (cot * opening).astype(bf16)
        ups[cols, :] = up
        dgate_ref[:, at] = (cot * attended * opening * (1.0 - opening)).astype(bf16)
        center = jnp.sum(jnp.transpose(up.astype(f32) * attended), axis=0, keepdims=True)
        cent[:, cols] = jnp.broadcast_to(center, (8, C))

    def grads(kb, carry):
        keys = kv_ref[rows_of(kb), 0:AD]
        values = kv_ref[rows_of(kb), AD : 2 * AD]
        dk = jnp.zeros((KB, AD), f32)
        dv = jnp.zeros((KB, AD), f32)
        for i in range(parts):
            cols = slice(i * width, (i + 1) * width)
            p = probs[rows_of(kb), cols] * low[0:1, cols]
            dp = lax.dot_general(values, ups[cols, :], NT, preferred_element_type=f32)
            ds = (p * (dp - cent[0:1, cols])).astype(bf16)
            dv = dv + lax.dot_general(p.astype(bf16), ups[cols, :], NN, preferred_element_type=f32)
            dk = dk + lax.dot_general(ds, qs[cols, :], NN, preferred_element_type=f32)
            dqt[:, cols] = dqt[:, cols] + lax.dot_general(
                keys, ds, TN, preferred_element_type=f32
            )
        dkv_ref[rows_of(kb), 0:AD] = dk
        dkv_ref[rows_of(kb), AD : 2 * AD] = dv
        return carry

    lax.fori_loop(0, blocks, grads, 0)

    def blank(kb, carry):
        dkv_ref[rows_of(kb), :] = jnp.zeros((KB, 2 * AD), f32)
        return carry

    lax.fori_loop(blocks, NKB, blank, 0)
    for g in range(GROUP):
        cols = slice(g * C, (g + 1) * C)
        dq_ref[:, g * AD : (g + 1) * AD] = (jnp.transpose(dqt[:, cols]) * scale).astype(bf16)


VM = pl.BlockSpec(memory_space=pltpu.VMEM)


def call(kernel, outs, args, scratch=(), collective=None):
    options = {"vmem_limit_bytes": VMEM_BIG}
    if collective is not None:
        options.update(collective_id=collective, has_side_effects=True)
    return pl.pallas_call(
        kernel,
        out_shape=tuple(jax.ShapeDtypeStruct(s, d) for s, d in outs),
        in_specs=[VM] * len(args),
        out_specs=tuple(VM for _ in outs),
        scratch_shapes=list(scratch),
        compiler_params=pltpu.CompilerParams(**options),
    )(*args)


SQ = (HEADS, DK, DK)


def per_device(
    delta_query, delta_key, delta_value, beta_logit, decay_input, decay_log, norm_gain,
    output_gate, delta_cotangent, attn_query, attn_key, attn_value, attn_gate, attn_cotangent,
):
    q, k, v = delta_query[0], delta_key[0], delta_value[0]
    gates = (beta_logit[0].T, decay_input[0].T, decay_log[:, None])
    wide = (C, HEADS * DK)
    dma = pltpu.SemaphoreType.DMA((N,))

    kv = jnp.concatenate([attn_key[0], attn_value[0]], axis=-1)
    kv_all = lax.all_gather(kv, "ctx", axis=0, tiled=True)

    inv, w, u0, m, off = call(
        chunk_kernel,
        [(SQ, f32), (SQ, f32), (SQ, f32), (SQ, bf16), ((N, SROWS + 8, DK), f32)],
        (k, v) + gates,
    )
    m_all, keep_all, state = call(
        forward_exchange,
        [((N, DK, DK), bf16), ((N, 8, DK), f32), ((N, SROWS, DK), f32)],
        (m, off),
        [pltpu.VMEM((N, SROWS + 8, DK), f32), pltpu.VMEM((N, SROWS, DK), f32)] + [dma] * 6,
        collective=1,
    )
    kv_all, state = lax.optimization_barrier((kv_all, state))
    flat = (C, GROUP * AD)
    attn_out, attn_dq, attn_dgate, dkv = call(
        attention_kernel,
        [(flat, bf16), (flat, bf16), (flat, bf16), ((LENGTH, 2 * AD), f32)],
        (attn_query[0], attn_gate[0], attn_cotangent[0], kv_all),
        [
            pltpu.VMEM((ROWS, AD), bf16),
            pltpu.VMEM((ROWS, AD), bf16),
            pltpu.VMEM((LENGTH, ROWS), f32),
            pltpu.VMEM((AD, ROWS), f32),
            pltpu.VMEM((AD, ROWS), f32),
            pltpu.VMEM((8, ROWS), f32),
            pltpu.VMEM((8, ROWS), f32),
            pltpu.VMEM((8, ROWS), f32),
        ],
    )
    dkv, state = lax.optimization_barrier((dkv, state))
    own = lax.psum_scatter(dkv, "ctx", scatter_dimension=0, tiled=True)

    state = state.reshape(SQ)
    out, dgate, dgain, u, do, dul, dsl = call(
        output_kernel,
        [(wide, bf16), (wide, bf16), ((1, DK), f32), (SQ, f32), (SQ, f32), (SQ, f32), (SQ, f32)],
        (state, q, k, w, u0) + gates + (norm_gain[None], output_gate[0], delta_cotangent[0]),
    )
    (dstate,) = call(
        backward_exchange,
        [((N, SROWS, DK), f32)],
        (m_all, keep_all, dsl.reshape(N, SROWS, DK)),
        [pltpu.VMEM((N, SROWS, DK), f32), pltpu.VMEM((N, SROWS, DK), f32)] + [dma] * 4,
        collective=2,
    )
    pair = (2 * HEADS, DK)
    rows = (HEADS, C)
    dq, dk, dv, dbl, ddi, sums = call(
        gradient_kernel,
        [(wide, bf16), (wide, bf16), (wide, bf16), (rows, f32), (rows, f32), (pair, f32)],
        (state, dstate.reshape(SQ), q, k, v, inv, u, do, dul) + gates + (dgain,),
    )
    (sums,) = call(
        sum_kernel,
        [(pair, f32)],
        (sums,),
        [pltpu.VMEM((N,) + pair, f32), pltpu.VMEM(pair, f32), pltpu.VMEM((3,) + pair, f32)]
        + [dma] * 2
        + [pltpu.SemaphoreType.DMA((3,))] * 2,
        collective=3,
    )
    log_grad, gain_grad = sums[:HEADS, 0], sums[HEADS]
    return (
        out[None], dq[None], dk[None], dv[None], dbl.T[None], ddi.T[None], log_grad, gain_grad,
        dgate[None], attn_out[None], attn_dq[None],
        own[:, :AD].astype(bf16)[None], own[:, AD:].astype(bf16)[None], attn_dgate[None],
    )


def solution(mesh):
    split3 = P("section", "ctx", "head")
    in_specs = (split3,) * 5 + (P("head"), P()) + (split3,) * 7
    out_specs = (split3,) * 6 + (P("head"), P()) + (split3,) * 6
    return jax.shard_map(
        per_device, mesh=mesh, in_specs=in_specs, out_specs=out_specs, check_vma=False
    )
```

time: 1360 us -> 207 us (0.15); the launches traced: 1340 us -> 206 us
  matrix products: 376 us -> 0 us
  starting transfers between devices: 334 us -> 0.08 us
  blocking collectives: 281 us -> 0 us
  local copies, waits for them, and re-layouts: 163 us -> 4.47 us
  Pallas kernels: 0 us -> 142 us
  waiting for transfers between devices: 117 us -> 42.7 us
  other arithmetic: 50.2 us -> 2.5 us
    dot_general x269 -> x0, matrix products: 376 us -> none  [the longest x34 93.4 us: compose(): jnp.einsum('hij,hjk->hik', earlier[1], later[0], precision=HIGHEST)]
    ppermute x31 -> x0, starting transfers between devices: 334 us -> none  [passed_along(): return lax.ppermute(block, axis, route)]
    psum x2 -> x0, blocking collectives: 281 us -> none  [the longest x1 166 us: per_device(): decay_log_grad = lax.psum(gradients[6], ('ctx', 'section'))]
    pallas_call x0 -> x7, Pallas kernels: none -> 142 us  [call(): pl.pallas_call(kernel, out_shape=tuple((jax.ShapeDtypeStruct(s, d) for s,...]
    dynamic_slice x88 -> x0, local copies, waits for them, and re-layouts: 54.8 us -> none  [the longest x64 40.7 us: lap(): new = combine(before, jax.tree.map(lambda part: part[at], everything))]
    ppermute x31 -> x0, waiting for transfers between devices: 53.2 us -> none  [passed_along(): return lax.ppermute(block, axis, route)]
    all_gather x4 -> x1, waiting for transfers between devices: 62.4 us -> 13.4 us  [per_device(): kv_all = lax.all_gather(kv, 'ctx', axis=0, tiled=True)]
    while x380 -> x0, local copies, waits for them, and re-layouts: 44.3 us -> none
  transfers between devices with their start and end apart: 36 -> 2, of which waited for: 33 -> 2; matrix products, arithmetic and copies ran while one was open for 16% -> 2% of each run, Pallas kernels for 0% -> 64%
where the time goes in v1:
time: 207 us; the launch traced here: 206 us
  Pallas kernels  142 us (69%)
  waiting for transfers between devices  42.7 us (21%)
  between operations  14.1 us (7%)
  local copies, waits for them, and re-layouts  4.47 us (2%)
  other arithmetic  2.5 us (1%)
    pallas_call x7, Pallas kernels, call(): pl.pallas_call(kernel, out_shape=tuple((jax.ShapeDtypeStruct(s, d) for s,...  142 us
    reduce_scatter x1, waiting for transfers between devices, per_device(): own = lax.psum_scatter(dkv, 'ctx', scatter_dimension=0, tiled=True)  29.2 us
    all_gather x1, waiting for transfers between devices, per_device(): kv_all = lax.all_gather(kv, 'ctx', axis=0, tiled=True)  13.4 us
  transfers between devices with their start and end apart: 2, of which 2 were waited for; matrix products, arithmetic and copies ran while one was open for 2% of the time, Pallas kernels for 64%

profile of v1, /device:TPU:0, one launch (start us, length us, event | category | flops | bytes accessed | tf_op | source)
XLA Modules:
  0.0 206.2 jit_solution(7302473344064354636)
XLA Ops:
  7.2 0.0 all-gather.2.cloned.1.call-start
  7.2 1.5 pad_maximum_fusion
  8.8 0.0 all-gather.2.cloned.1.call-update
  8.8 0.0 reduce-scatter.2.cloned.1.call-start
  8.8 1.3 copy.31.dl_ref
  10.2 8.0 %shard_map.245 = (f32[8,128,128]{2,1,0:T(8,128)}, f32[8,128,128]{2,1,0:T(8,128)}, f32[8,128,128]{2,1,0:T(8,128)}, bf16[8,128,128]{2,1,0:T(8,128)(2,1)}, f32[32,40,128]{2,1,0:T(8,128)}) custom-call(bf16[128,1024]{1,0:T(8,128)(2,1)} %bitcast.41, bf16[128,1024]{1,0:T(8,128)(2,1)} %bitcast.49, f32[8,128]{1,0:T(8,128)} %bitcast.59, f32[8,128]{1,0:T(8,128)} %bitcast.62, ...), custom_call_target="tpu_custom_call" | custom-call | tf_op jit(solution)/shard_map/pallas_call | solution.py:518
  18.2 43.9 %shard_map.246 = (bf16[32,128,128]{2,1,0:T(8,128)(2,1)}, f32[32,8,128]{2,1,0:T(8,128)}, f32[32,32,128]{2,1,0:T(8,128)}) custom-call(bf16[8,128,128]{2,1,0:T(8,128)(2,1)} %get-tuple-element.43.m_ref, f32[32,40,128]{2,1,0:T(8,128)} %get-tuple-element.44.o_ref), custom_call_target="tpu_custom_call" | custom-call | tf_op jit(solution)/shard_map/pallas_call | solution.py:518
  62.1 13.4 %all-gather.2.cloned.1.call-done.kv_ref = bf16[4096,512]{1,0:T(8,128)(2,1)} async-done(((bf16[128,512]{1,0:T(8,128)(2,1)}), bf16[4096,512]{1,0:T(8,128)(2,1)}) %all-gather.2.cloned.1.call-update) | async-done | bytes 4194320 | tf_op jit(solution)/shard_map/all_gather | solution.py:541
  75.5 11.0 %shard_map.247 = (bf16[128,2048]{1,0:T(8,128)(2,1)}, bf16[128,2048]{1,0:T(8,128)(2,1)}, bf16[128,2048]{1,0:T(8,128)(2,1)}, f32[4096,512]{1,0:T(8,128)}) custom-call(bf16[128,2048]{1,0:T(8,128)(2,1)} %bitcast.52, bf16[128,2048]{1,0:T(8,128)(2,1)} %bitcast.53, bf16[128,2048]{1,0:T(8,128)(2,1)} %bitcast.54, bf16[4096,512]{1,0:T(8,128)(2,1)} %all-gather.2.cloned.1.call-done.kv_ref), custom_call_target="tpu_custom_call" | custom-call | tf_op jit(solution)/shard_map/pallas_call | solution.py:518
  86.6 0.0 reduce-scatter.2.cloned.1.call-update
  86.6 9.4 %shard_map.248 = (bf16[128,1024]{1,0:T(8,128)(2,1)}, bf16[128,1024]{1,0:T(8,128)(2,1)}, f32[1,128]{1,0:T(1,128)}, f32[8,128,128]{2,1,0:T(8,128)}, f32[8,128,128]...) custom-call(f32[8,128,128]{2,1,0:T(8,128)} %bitcast.45, bf16[128,1024]{1,0:T(8,128)(2,1)} %bitcast.47, ...), custom_call_target="tpu_custom_call" | custom-call | tf_op jit(solution)/shard_map/pallas_call | solution.py:518
  96.0 43.2 %shard_map.249 = f32[32,32,128]{2,1,0:T(8,128)} custom-call(bf16[32,128,128]{2,1,0:T(8,128)(2,1)} %get-tuple-element.53.mall, f32[32,8,128]{2,1,0:T(8,128)} %get-tuple-element.54.eall, f32[32,32,128]{2,1,0:T(8,128)} %bitcast.51), custom_call_target="tpu_custom_call" | custom-call | tf_op jit(solution)/shard_map/pallas_call | solution.py:518
  139.2 10.8 %shard_map.250 = (bf16[128,1024]{1,0:T(8,128)(2,1)}, bf16[128,1024]{1,0:T(8,128)(2,1)}, bf16[128,1024]{1,0:T(8,128)(2,1)}, f32[8,128]{1,0:T(8,128)}, f32[8,128]{1,0:T(8,128)}, /*index=5*/f32[16,128]{1,0:T(8,128)}) custom-call(f32[8,128,128]{2,1,0:T(8,128)} %bitcast.46, f32[8,128,128]{2,1,0:T(8,128)} %bitcast.44, bf16[128,1024]{1,0:T(8,128)(2,1)} %bitcast.48, ...), custom_call_target="tpu_custom_call" | custom-call | tf_op jit(solution)/shard_map/pallas_call | solution.py:518
  150.0 16.0 %shard_map.251 = f32[16,128]{1,0:T(8,128)} custom-call(f32[16,128]{1,0:T(8,128)} %get-tuple-element.66.x_ref), custom_call_target="tpu_custom_call" | custom-call | tf_op jit(solution)/shard_map/pallas_call | solution.py:518
  166.0 1.3 slice_reduce_fusion
  167.3 1.2 slice_bitcast_fusion.2
  168.5 29.2 %reduce-scatter.2.cloned.1.call-done = f32[128,512]{1,0:T(8,128)} async-done(((f32[4096,512]{1,0:T(8,128)}), f32[128,512]{1,0:T(8,128)}) %reduce-scatter.2.cloned.1.call-update) | async-done | bytes 262160 | tf_op jit(solution)/shard_map/reduce_scatter | solution.py:573
  197.7 1.0 convert.4
  198.7 0.7 slice_bitcast_fusion
Async XLA Ops:
  7.2 68.4 %all-gather.2.cloned.1.call-start = ((), (), s32[]{:S(2)}) async-start(), calls=%async_computation.1 | async-start | bytes 4325376 | tf_op jit(solution)/shard_map/all_gather | solution.py:541
  8.8 188.9 %reduce-scatter.2.cloned.1.call-start = ((), (), s32[]{:S(2)}) async-start(), calls=%async_computation.2 | async-start | bytes 8650752 | tf_op jit(solution)/shard_map/reduce_scatter | solution.py:573
Sparse Core Ops, SparseCore 0:
  10.8 64.6 all-gather.1
  86.7 110.9 reduce-scatter.1

commit v2 on v1

--- a/solution.py
+++ b/solution.py
@@ -23,6 +23,8 @@
 NKB = LENGTH // KB
 QUARTERS = N // HEADS
 SROWS = DK // QUARTERS
+KEEP = 16
+CHIPS = N // 2
 VMEM_BIG = 60 * 1024 * 1024
 
 NT = (((1,), (1,)), ((), ()))
@@ -68,7 +70,11 @@
 def gates_of(bl_ref, di_ref, dl_ref):
     beta = 1.0 / (1.0 + jnp.exp(-bl_ref[...]))
     a = di_ref[...]
-    rate = -jnp.exp(dl_ref[...])
+    head = lax.broadcasted_iota(jnp.int32, a.shape, 0)
+    logs = jnp.zeros(a.shape, f32)
+    for h in range(HEADS):
+        logs = jnp.where(head == h, dl_ref[h], logs)
+    rate = -jnp.exp(logs)
     soft = jnp.maximum(a, 0.0) + jnp.log1p(jnp.exp(-jnp.abs(a)))
     g = jnp.maximum(rate * soft, -104.0)
     r, c = iotas()
@@ -119,11 +125,16 @@
             w_ref[h] = W
             u0_ref[h] = U0
             m_ref[h] = (-d3(W, Kt, TN)).astype(bf16)
-            off = d3(U0, Kt, TN)
-            keep = jnp.broadcast_to(jnp.exp(cl), (8, DK))
+            off = d3(U0, Kt, TN).astype(bf16)
+            keep = jnp.broadcast_to(jnp.exp(cl), (KEEP, DK))
+            high = keep.astype(bf16)
+            mid = (keep - high.astype(f32)).astype(bf16)
+            last = keep - high.astype(f32) - mid.astype(f32)
+            row = lax.broadcasted_iota(jnp.int32, (KEEP, DK), 0)
+            terms = jnp.where(row == 0, high.astype(f32), jnp.where(row == 1, mid.astype(f32), last))
             for q in range(QUARTERS):
                 o_ref[h * QUARTERS + q, 0:SROWS, :] = off[q * SROWS : (q + 1) * SROWS, :]
-                o_ref[h * QUARTERS + q, SROWS : SROWS + 8, :] = keep
+                o_ref[h * QUARTERS + q, SROWS : SROWS + KEEP, :] = terms.astype(bf16)
 
 
 def greet(me):
@@ -150,62 +161,98 @@
     )
 
 
-def advanced(S, M, dims):
-    hi, lo = split(S)
-    both = jnp.concatenate([hi.astype(f32), lo.astype(f32)], axis=0).astype(bf16)
-    out = lax.dot_general(both, M, dims, preferred_element_type=f32)
-    return out[:SROWS] + out[SROWS:]
-
-
 def forward_exchange(
-    m_ref, o_ref, mall, eall, srecv, oall, sbuf, m_send, m_recv, o_send, o_recv, s_send, s_recv
+    m_ref, o_ref, mall, eall, srecv, oall, sbuf,
+    m_send, m_recv, f_send, f_recv, o_send, o_recv, s_send, s_recv,
 ):
     me = lax.axis_index("ctx")
+    core = lax.rem(me, 2)
+    chip = me // 2
+    mate = chip * 2 + 1 - core
     greet(me)
 
-    def send(p, carry):
+    def to_core(p):
+        return lax.rem(chip + p, CHIPS) * 2 + core
+
+    def send_map(p, carry):
+        peer = to_core(p)
+        remote(m_ref.at[peer // QUARTERS], mall.at[me], m_send.at[p], m_recv.at[me], peer).start()
+        return carry
+
+    def send_offset(p, carry):
         peer = lax.rem(me + p, N)
-        remote(m_ref.at[peer // QUARTERS], mall.at[me], m_send.at[p], m_recv.at[me], peer).start()
         remote(o_ref.at[peer], oall.at[me], o_send.at[p], o_recv.at[me], peer).start()
         return carry
 
-    lax.fori_loop(1, N, send, 0)
+    lax.fori_loop(1, CHIPS, send_map, 0)
+    lax.fori_loop(1, N, send_offset, 0)
     mall[me] = m_ref[me // QUARTERS]
     oall[me] = o_ref[me]
 
-    def step(s, S):
+    def hand_over(source):
+        return remote(mall.at[source], mall.at[source], f_send.at[source], f_recv.at[source], mate)
+
+    def arrive(c):
+        source = 2 * c + core
+
+        @pl.when(source != me)
+        def _():
+            remote(m_ref.at[0], mall.at[source], m_send.at[0], m_recv.at[source], source).wait_recv()
+
+        hand_over(source).start()
+
+    def advance(s, S):
         @pl.when(s != me)
         def _():
-            remote(m_ref.at[0], mall.at[s], m_send.at[0], m_recv.at[s], s).wait_recv()
             remote(o_ref.at[0], oall.at[s], o_send.at[0], o_recv.at[s], s).wait_recv()
 
-        sbuf[s] = S
+        sbuf[s] = S.astype(bf16)
 
         @pl.when(s != me)
         def _():
             remote(sbuf.at[s], srecv.at[me], s_send.at[s], s_recv.at[me], s).start()
 
-        keep = oall[s, SROWS : SROWS + 8, :]
-        eall[s] = keep
-        return keep[0:1, :] * S + advanced(S, mall[s], NN) + oall[s, 0:SROWS, :]
-
-    lax.fori_loop(0, N, step, jnp.zeros((SROWS, DK), f32))
+        terms = oall[s, SROWS : SROWS + KEEP, :].astype(f32)
+        keep = terms[0:1] + (terms[1:2] + terms[2:3])
+        eall[s] = jnp.broadcast_to(keep, (8, DK))
+        return keep * S + d1(S, mall[s], NN) + oall[s, 0:SROWS, :].astype(f32)
+
+    def pair(c, S):
+        other = 2 * c + 1 - core
+        hand_over(other).wait_recv()
+        return advance(2 * c + 1, advance(2 * c, S))
+
+    def step(c, S):
+        arrive(c)
+        return pair(c - 1, S)
+
+    arrive(0)
+    S = lax.fori_loop(1, CHIPS, step, jnp.zeros((SROWS, DK), f32))
+    pair(CHIPS - 1, S)
     srecv[me] = sbuf[me]
+
+    def finish_map(p, carry):
+        peer = to_core(p)
+        remote(m_ref.at[0], mall.at[me], m_send.at[p], m_recv.at[me], peer).wait_send()
+        return carry
+
+    def finish_pass(c, carry):
+        hand_over(2 * c + core).wait_send()
+        return carry
 
     def finish(p, carry):
         peer = lax.rem(me + p, N)
-        remote(m_ref.at[0], mall.at[me], m_send.at[p], m_recv.at[me], peer).wait_send()
         remote(o_ref.at[0], oall.at[me], o_send.at[p], o_recv.at[me], peer).wait_send()
         remote(sbuf.at[peer], srecv.at[me], s_send.at[peer], s_recv.at[me], peer).wait_send()
         remote(sbuf.at[peer], srecv.at[peer], s_send.at[peer], s_recv.at[peer], peer).wait_recv()
         return carry
 
+    lax.fori_loop(1, CHIPS, finish_map, 0)
+    lax.fori_loop(0, CHIPS, finish_pass, 0)
     lax.fori_loop(1, N, finish, 0)
 
 
-def backward_exchange(
-    mall, eall, l_ref, srecv, lall, sbuf, l_send, l_recv, s_send, s_recv
-):
+def backward_exchange(mall, eall, l_ref, srecv, lall, sbuf, l_send, l_recv, s_send, s_recv):
     me = lax.axis_index("ctx")
     greet(me)
 
@@ -219,14 +266,14 @@
 
     def step(k, S):
         s = N - 1 - k
-        sbuf[s] = S
+        sbuf[s] = S.astype(bf16)
 
         @pl.when(s != me)
         def _():
             remote(sbuf.at[s], srecv.at[me], s_send.at[s], s_recv.at[me], s).start()
             remote(l_ref.at[0], lall.at[s], l_send.at[0], l_recv.at[s], s).wait_recv()
 
-        return eall[s, 0:1, :] * S + advanced(S, mall[s], NT) + lall[s]
+        return eall[s, 0:1, :] * S + d1(S, mall[s], NT) + lall[s].astype(f32)
 
     lax.fori_loop(0, N, step, jnp.zeros((SROWS, DK), f32))
     srecv[me] = sbuf[me]
@@ -252,7 +299,7 @@
         at = slice(h * DK, (h + 1) * DK)
         Q = unit(head_cols(q_ref, h))[0] * DK**-0.5
         K = unit(head_cols(k_ref, h))[0]
-        S, W = s_ref[h], w_ref[h]
+        S, W = s_ref[h].astype(f32), w_ref[h]
         cc = cols[:, h : h + 1]
         ec = jnp.exp(cc)
         F = fade(cc, rows[h : h + 1, :])
@@ -274,7 +321,7 @@
         u_ref[h] = U
         do_ref[h] = dO
         dul_ref[h] = dUl
-        dsl_ref[h] = d3(ec * dO, Q, TN) - d3(dUl, W, TN)
+        dsl_ref[h] = (d3(ec * dO, Q, TN) - d3(dUl, W, TN)).astype(bf16)
     dgain_ref[...] = gain_sum
 
 
@@ -297,7 +344,8 @@
         Q = Q0 * DK**-0.5
         K, rk = unit(xk)
         V = head_cols(v_ref, h)
-        S, dS, I, U, dO, dUl = s_ref[h], ds_ref[h], n_ref[h], u_ref[h], do_ref[h], dul_ref[h]
+        S, dS = s_ref[h].astype(f32), ds_ref[h].astype(f32)
+        I, U, dO, dUl = n_ref[h], u_ref[h], do_ref[h], dul_ref[h]
         b, cc = beta[:, h : h + 1], cols[:, h : h + 1]
         ec = jnp.exp(cc)
         F = fade(cc, rows[h : h + 1, :])
@@ -350,71 +398,53 @@
     sums_ref[HEADS : 2 * HEADS, :] = jnp.broadcast_to(dgain_ref[...], (HEADS, DK))
 
 
-def sum_kernel(x_ref, out_ref, every, part, others, send1, recv1, send2, recv2):
+def attention_kernel(
+    q_ref, gate_ref, cot_ref, kv_ref, x_ref,
+    out_ref, dq_ref, dgate_ref, dk_ref, dv_ref, sums_ref,
+    qs, ups, probs, att, dqt, top, low, cent,
+    block, keep, give, got, both, taken, total, pairs, every, part, others,
+    g_send, g_recv, b_send, b_recv, p_send, p_recv, e_send, e_recv, a_send, a_recv,
+):
     me, head, section = (lax.axis_index(a) for a in ("ctx", "head", "section"))
+    core = lax.rem(me, 2)
+    chip = me // 2
+    mate = chip * 2 + 1 - core
     barrier = pltpu.get_barrier_semaphore()
 
+    def to_core(p):
+        return lax.rem(chip + p, CHIPS) * 2 + core
+
     def hello(p, carry):
-        pl.semaphore_signal(
-            barrier, inc=1, device_id={"ctx": lax.rem(me + p, N)}, device_id_type=MESH
-        )
-        return carry
-
-    lax.fori_loop(1, N, hello, 0)
+        pl.semaphore_signal(barrier, inc=1, device_id={"ctx": to_core(p)}, device_id_type=MESH)
+        return carry
+
     turns = ((0, 1), (1, 0), (1, 1))
 
-    def aside(dh, ds):
+    def aside(i):
+        dh, ds = turns[i]
         return {"head": lax.rem(head + dh, 2), "section": lax.rem(section + ds, 2)}
 
-    for dh, ds in turns:
-        pl.semaphore_signal(barrier, inc=1, device_id=aside(dh, ds), device_id_type=MESH)
-    pl.semaphore_wait(barrier, N + 2)
-
-    def send(p, carry):
-        peer = lax.rem(me + p, N)
-        remote(x_ref, every.at[me], send1.at[p], recv1.at[me], peer).start()
-        return carry
-
-    lax.fori_loop(1, N, send, 0)
-    every[me] = x_ref[...]
-
-    def finish(p, carry):
-        peer = lax.rem(me + p, N)
-        remote(x_ref, every.at[me], send1.at[p], recv1.at[me], peer).wait_send()
-        remote(x_ref, every.at[peer], send1.at[p], recv1.at[peer], peer).wait_recv()
-        return carry
-
-    lax.fori_loop(1, N, finish, 0)
-    part[...] = jnp.sum(every[...], axis=0)
-    copies = [
-        pltpu.make_async_remote_copy(
-            src_ref=part,
+    lax.fori_loop(1, CHIPS, hello, 0)
+    pl.semaphore_signal(barrier, inc=1, device_id={"ctx": mate}, device_id_type=MESH)
+    for i in range(3):
+        pl.semaphore_signal(barrier, inc=1, device_id=aside(i), device_id_type=MESH)
+
+    def pair_copy():
+        return remote(x_ref, pairs, p_send, p_recv, mate)
+
+    def every_copy(p, source):
+        return remote(part, every.at[source], e_send.at[p], e_recv.at[source], to_core(p))
+
+    def aside_copy(i):
+        return pltpu.make_async_remote_copy(
+            src_ref=total,
             dst_ref=others.at[i],
-            send_sem=send2.at[i],
-            recv_sem=recv2.at[i],
-            device_id=aside(dh, ds),
+            send_sem=a_send.at[i],
+            recv_sem=a_recv.at[i],
+            device_id=aside(i),
             device_id_type=MESH,
         )
-        for i, (dh, ds) in enumerate(turns)
-    ]
-    for copy in copies:
-        copy.start()
-    for copy in copies:
-        copy.wait()
-    same = slice(0, HEADS)
-    gain = slice(HEADS, 2 * HEADS)
-    out_ref[same, :] = part[same, :] + others[0, same, :]
-    out_ref[gain, :] = (part[gain, :] + others[0, gain, :]) + (
-        others[1, gain, :] + others[2, gain, :]
-    )
-
-
-def attention_kernel(
-    q_ref, gate_ref, cot_ref, kv_ref,
-    out_ref, dq_ref, dgate_ref, dkv_ref,
-    qs, ups, probs, att, dqt, top, low, cent,
-):
-    me = lax.axis_index("ctx")
+
     blocks = me // (KB // C) + 1
     scale = AD**-0.5
     width = 256
@@ -461,7 +491,18 @@
             )
         return carry
 
+    pl.semaphore_wait(barrier, CHIPS + 3)
+    pair_copy().start()
     lax.fori_loop(0, blocks, weigh, 0)
+    pair_copy().wait()
+    part[...] = x_ref[...] + pairs[...]
+
+    def send_part(p, carry):
+        every_copy(p, chip).start()
+        return carry
+
+    lax.fori_loop(1, CHIPS, send_part, 0)
+    every[chip] = part[...]
     share = 1.0 / jnp.sum(low[...], axis=0, keepdims=True)
     low[...] = jnp.broadcast_to(share, (8, ROWS))
     for g in range(GROUP):
@@ -477,7 +518,13 @@
         center = jnp.sum(jnp.transpose(up.astype(f32) * attended), axis=0, keepdims=True)
         cent[:, cols] = jnp.broadcast_to(center, (8, C))
 
-    def grads(kb, carry):
+    def give_copy(c):
+        return remote(give.at[c], got.at[c], g_send.at[c], g_recv.at[c], mate)
+
+    def both_copy(c, source):
+        return remote(both.at[c], taken.at[source], b_send.at[c], b_recv.at[source], 2 * c + core)
+
+    def grads(kb):
         keys = kv_ref[rows_of(kb), 0:AD]
         values = kv_ref[rows_of(kb), AD : 2 * AD]
         dk = jnp.zeros((KB, AD), f32)
@@ -492,23 +539,92 @@
             dqt[:, cols] = dqt[:, cols] + lax.dot_general(
                 keys, ds, TN, preferred_element_type=f32
             )
-        dkv_ref[rows_of(kb), 0:AD] = dk
-        dkv_ref[rows_of(kb), AD : 2 * AD] = dv
-        return carry
-
-    lax.fori_loop(0, blocks, grads, 0)
-
-    def blank(kb, carry):
-        dkv_ref[rows_of(kb), :] = jnp.zeros((KB, 2 * AD), f32)
-        return carry
-
-    lax.fori_loop(blocks, NKB, blank, 0)
+        block[:, 0:AD] = dk
+        block[:, AD : 2 * AD] = dv
+        for u in range(KB // (2 * C)):
+            c = kb * (KB // (2 * C)) + u
+            mine = pl.multiple_of((2 * u + core) * C, C)
+            theirs = pl.multiple_of((2 * u + 1 - core) * C, C)
+            keep[c] = block[pl.ds(mine, C), :]
+            give[c] = block[pl.ds(theirs, C), :].astype(bf16)
+
+            @pl.when(c <= chip)
+            def _():
+                give_copy(c).start()
+
+    def forward(kb):
+        for u in range(KB // (2 * C)):
+            c = kb * (KB // (2 * C)) + u
+
+            @pl.when(c <= chip)
+            def _():
+                give_copy(c).wait_recv()
+                both[c] = (keep[c] + got[c].astype(f32)).astype(bf16)
+
+            @pl.when(c < chip)
+            def _():
+                both_copy(c, chip).start()
+
+    def later(t, carry):
+        kb = blocks - 1 - t
+        grads(kb)
+        forward(kb + 1)
+        return carry
+
+    grads(blocks - 1)
+    lax.fori_loop(1, blocks, later, 0)
+    forward(0)
+
+    def take_part(p, carry):
+        source = lax.rem(chip + p, CHIPS)
+        every_copy(p, chip).wait_send()
+        every_copy(p, source).wait_recv()
+        return carry
+
+    lax.fori_loop(1, CHIPS, take_part, 0)
+    total[...] = jnp.sum(every[...], axis=0)
+    for i in range(3):
+        aside_copy(i).start()
+
     for g in range(GROUP):
         cols = slice(g * C, (g + 1) * C)
         dq_ref[:, g * AD : (g + 1) * AD] = (jnp.transpose(dqt[:, cols]) * scale).astype(bf16)
 
+    keep[chip] = keep[chip] + got[chip].astype(f32)
+
+    def collect(t, carry):
+        source = CHIPS - 1 - t
+        both_copy(source, source).wait_recv()
+        keep[chip] = keep[chip] + taken[source].astype(f32)
+        return carry
+
+    def sent(c, carry):
+        give_copy(c).wait_send()
+
+        @pl.when(c < chip)
+        def _():
+            both_copy(c, chip).wait_send()
+
+        return carry
+
+    lax.fori_loop(0, CHIPS - 1 - chip, collect, 0)
+    dk_ref[...] = keep[chip, :, 0:AD].astype(bf16)
+    dv_ref[...] = keep[chip, :, AD : 2 * AD].astype(bf16)
+    lax.fori_loop(0, chip + 1, sent, 0)
+    for i in range(3):
+        aside_copy(i).wait()
+    same = slice(0, HEADS)
+    gain = slice(HEADS, 2 * HEADS)
+    sums_ref[same, :] = total[same, :] + others[0, same, :]
+    sums_ref[gain, :] = (total[gain, :] + others[0, gain, :]) + (
+        others[1, gain, :] + others[2, gain, :]
+    )
+
 
 VM = pl.BlockSpec(memory_space=pltpu.VMEM)
+
+
+SM = pl.BlockSpec(memory_space=pltpu.SMEM)
 
 
 def call(kernel, outs, args, scratch=(), collective=None):
@@ -518,7 +634,7 @@
     return pl.pallas_call(
         kernel,
         out_shape=tuple(jax.ShapeDtypeStruct(s, d) for s, d in outs),
-        in_specs=[VM] * len(args),
+        in_specs=[SM if x.ndim == 1 else VM for x in args],
         out_specs=tuple(VM for _ in outs),
         scratch_shapes=list(scratch),
         compiler_params=pltpu.CompilerParams(**options),
@@ -533,79 +649,75 @@
     output_gate, delta_cotangent, attn_query, attn_key, attn_value, attn_gate, attn_cotangent,
 ):
     q, k, v = delta_query[0], delta_key[0], delta_value[0]
-    gates = (beta_logit[0].T, decay_input[0].T, decay_log[:, None])
+    gates = (beta_logit[0].T, decay_input[0].T, decay_log)
     wide = (C, HEADS * DK)
-    dma = pltpu.SemaphoreType.DMA((N,))
+    rows = (HEADS, C)
+    pair = (2 * HEADS, DK)
+    states = (N, SROWS, DK)
+
+    def vm(shape, dtype=f32):
+        return pltpu.VMEM(shape, dtype)
+
+    def dma(count):
+        return pltpu.SemaphoreType.DMA((count,))
 
     kv = jnp.concatenate([attn_key[0], attn_value[0]], axis=-1)
     kv_all = lax.all_gather(kv, "ctx", axis=0, tiled=True)
 
     inv, w, u0, m, off = call(
         chunk_kernel,
-        [(SQ, f32), (SQ, f32), (SQ, f32), (SQ, bf16), ((N, SROWS + 8, DK), f32)],
+        [(SQ, f32), (SQ, f32), (SQ, f32), (SQ, bf16), ((N, SROWS + KEEP, DK), bf16)],
         (k, v) + gates,
     )
     m_all, keep_all, state = call(
         forward_exchange,
-        [((N, DK, DK), bf16), ((N, 8, DK), f32), ((N, SROWS, DK), f32)],
+        [((N, DK, DK), bf16), ((N, 8, DK), f32), (states, bf16)],
         (m, off),
-        [pltpu.VMEM((N, SROWS + 8, DK), f32), pltpu.VMEM((N, SROWS, DK), f32)] + [dma] * 6,
+        [vm((N, SROWS + KEEP, DK), bf16), vm(states, bf16)] + [dma(N)] * 8,
         collective=1,
     )
-    kv_all, state = lax.optimization_barrier((kv_all, state))
-    flat = (C, GROUP * AD)
-    attn_out, attn_dq, attn_dgate, dkv = call(
-        attention_kernel,
-        [(flat, bf16), (flat, bf16), (flat, bf16), ((LENGTH, 2 * AD), f32)],
-        (attn_query[0], attn_gate[0], attn_cotangent[0], kv_all),
-        [
-            pltpu.VMEM((ROWS, AD), bf16),
-            pltpu.VMEM((ROWS, AD), bf16),
-            pltpu.VMEM((LENGTH, ROWS), f32),
-            pltpu.VMEM((AD, ROWS), f32),
-            pltpu.VMEM((AD, ROWS), f32),
-            pltpu.VMEM((8, ROWS), f32),
-            pltpu.VMEM((8, ROWS), f32),
-            pltpu.VMEM((8, ROWS), f32),
-        ],
-    )
-    dkv, state = lax.optimization_barrier((dkv, state))
-    own = lax.psum_scatter(dkv, "ctx", scatter_dimension=0, tiled=True)
-
     state = state.reshape(SQ)
     out, dgate, dgain, u, do, dul, dsl = call(
         output_kernel,
-        [(wide, bf16), (wide, bf16), ((1, DK), f32), (SQ, f32), (SQ, f32), (SQ, f32), (SQ, f32)],
+        [(wide, bf16), (wide, bf16), ((1, DK), f32), (SQ, f32), (SQ, f32), (SQ, f32), (SQ, bf16)],
         (state, q, k, w, u0) + gates + (norm_gain[None], output_gate[0], delta_cotangent[0]),
     )
     (dstate,) = call(
         backward_exchange,
-        [((N, SROWS, DK), f32)],
-        (m_all, keep_all, dsl.reshape(N, SROWS, DK)),
-        [pltpu.VMEM((N, SROWS, DK), f32), pltpu.VMEM((N, SROWS, DK), f32)] + [dma] * 4,
+        [(states, bf16)],
+        (m_all, keep_all, dsl.reshape(states)),
+        [vm(states, bf16), vm(states, bf16)] + [dma(N)] * 4,
         collective=2,
     )
-    pair = (2 * HEADS, DK)
-    rows = (HEADS, C)
     dq, dk, dv, dbl, ddi, sums = call(
         gradient_kernel,
         [(wide, bf16), (wide, bf16), (wide, bf16), (rows, f32), (rows, f32), (pair, f32)],
         (state, dstate.reshape(SQ), q, k, v, inv, u, do, dul) + gates + (dgain,),
     )
-    (sums,) = call(
-        sum_kernel,
-        [(pair, f32)],
-        (sums,),
-        [pltpu.VMEM((N,) + pair, f32), pltpu.VMEM(pair, f32), pltpu.VMEM((3,) + pair, f32)]
-        + [dma] * 2
-        + [pltpu.SemaphoreType.DMA((3,))] * 2,
+    flat = (C, GROUP * AD)
+    own = (C, AD)
+    blocks = (CHIPS, C, 2 * AD)
+    attn_out, attn_dq, attn_dgate, attn_dk, attn_dv, sums = call(
+        attention_kernel,
+        [(flat, bf16), (flat, bf16), (flat, bf16), (own, bf16), (own, bf16), (pair, f32)],
+        (attn_query[0], attn_gate[0], attn_cotangent[0], kv_all, sums),
+        [
+            vm((ROWS, AD), bf16), vm((ROWS, AD), bf16), vm((LENGTH, ROWS)),
+            vm((AD, ROWS)), vm((AD, ROWS)), vm((8, ROWS)), vm((8, ROWS)), vm((8, ROWS)),
+            vm((KB, 2 * AD)), vm(blocks), vm(blocks, bf16), vm(blocks, bf16),
+            vm(blocks, bf16), vm(blocks, bf16),
+            vm(pair), vm(pair), vm((CHIPS,) + pair), vm(pair), vm((3,) + pair),
+        ]
+        + [dma(CHIPS)] * 4
+        + [pltpu.SemaphoreType.DMA] * 2
+        + [dma(CHIPS)] * 2
+        + [dma(3)] * 2,
         collective=3,
     )
-    log_grad, gain_grad = sums[:HEADS, 0], sums[HEADS]
     return (
-        out[None], dq[None], dk[None], dv[None], dbl.T[None], ddi.T[None], log_grad, gain_grad,
-        dgate[None], attn_out[None], attn_dq[None],
-        own[:, :AD].astype(bf16)[None], own[:, AD:].astype(bf16)[None], attn_dgate[None],
+        out[None], dq[None], dk[None], dv[None], dbl.T[None], ddi.T[None],
+        sums[:HEADS, 0], sums[HEADS], dgate[None], attn_out[None], attn_dq[None],
+        attn_dk[None], attn_dv[None], attn_dgate[None],
     )
 
 

time: 207 us -> 161 us (0.78)
  waiting for transfers between devices: 42.7 us -> 0.03 us
  Pallas kernels: 142 us -> 133 us
  local copies, waits for them, and re-layouts: 4.47 us -> 11.1 us
    reduce_scatter x1 -> x0, waiting for transfers between devices: 29.2 us -> none  [per_device(): own = lax.psum_scatter(dkv, 'ctx', scatter_dimension=0, tiled=True)]
    all_gather x1, waiting for transfers between devices: 13.4 us -> 0.02 us  [per_device(): kv_all = lax.all_gather(kv, 'ctx', axis=0, tiled=True)]
    pallas_call x7 -> x6, Pallas kernels: 142 us -> 133 us  [call(): pl.pallas_call(kernel, out_shape=tuple((jax.ShapeDtypeStruct(s, d) for s,...]
    unnamed x0 -> x5, local copies, waits for them, and re-layouts: none -> 8.58 us
  transfers between devices with their start and end apart: 2 -> 1, of which waited for: 2 -> 0; matrix products, arithmetic and copies ran while one was open for 2% -> 0% of each run, Pallas kernels for 64% -> 54%
where the time goes in v2:
time: 161 us; the launch traced here: 159 us
  Pallas kernels  133 us (83%)
  between operations  14.1 us (9%)
  local copies, waits for them, and re-layouts  11.1 us (7%)
    pallas_call x6, Pallas kernels, call(): pl.pallas_call(kernel, out_shape=tuple((jax.ShapeDtypeStruct(s, d) for s,...  133 us
    unnamed x5, local copies, waits for them, and re-layouts  8.58 us
  transfers between devices with their start and end apart: 1, of which 0 were waited for; matrix products, arithmetic and copies ran while one was open for 0% of the time, Pallas kernels for 54%

profile of v2, /device:TPU:0, one launch (start us, length us, event | category | flops | bytes accessed | tf_op | source)
XLA Modules:
  0.0 159.3 jit_solution(15856886203272223129)
XLA Ops:
  7.2 0.0 all-gather.2.cloned.1.call-start
  7.2 1.5 pad_maximum_fusion
  8.8 0.0 all-gather.2.cloned.1.call-update
  8.8 7.9 %shard_map.245 = (f32[8,128,128]{2,1,0:T(8,128)}, f32[8,128,128]{2,1,0:T(8,128)}, f32[8,128,128]{2,1,0:T(8,128)}, bf16[8,128,128]{2,1,0:T(8,128)(2,1)}, bf16[32,48,128]{2,1,0:T(8,128)(2,1)}) custom-call(bf16[128,1024]{1,0:T(8,128)(2,1)} %bitcast.38, bf16[128,1024]{1,0:T(8,128)(2,1)} %bitcast.45, f32[8,128]{1,0:T(8,128)} %bitcast.61, f32[8,128]{1,0:T(8,128)} %bitcast.64, ...), custom_call_target="tpu_custom_call" | custom-call | tf_op jit(solution)/shard_map/pallas_call | solution.py:634
  16.7 34.4 %shard_map.246 = (bf16[32,128,128]{2,1,0:T(8,128)(2,1)}, f32[32,8,128]{2,1,0:T(8,128)}, bf16[32,32,128]{2,1,0:T(8,128)(2,1)}) custom-call(bf16[8,128,128]{2,1,0:T(8,128)(2,1)} %get-tuple-element.41.m_ref, bf16[32,48,128]{2,1,0:T(8,128)(2,1)} %get-tuple-element.42.o_ref), custom_call_target="tpu_custom_call" | custom-call | tf_op jit(solution)/shard_map/pallas_call | solution.py:634
  51.1 9.2 %shard_map.247 = (bf16[128,1024]{1,0:T(8,128)(2,1)}, bf16[128,1024]{1,0:T(8,128)(2,1)}, f32[1,128]{1,0:T(1,128)}, f32[8,128,128]{2,1,0:T(8,128)}, f32[8,128,128]...) custom-call(bf16[8,128,128]{2,1,0:T(8,128)(2,1)} %bitcast.43, bf16[128,1024]{1,0:T(8,128)(2,1)} %bitcast.41, ...), custom_call_target="tpu_custom_call" | custom-call | tf_op jit(solution)/shard_map/pallas_call | solution.py:634
  60.3 23.9 %shard_map.248 = bf16[32,32,128]{2,1,0:T(8,128)(2,1)} custom-call(bf16[32,128,128]{2,1,0:T(8,128)(2,1)} %get-tuple-element.47.mall, f32[32,8,128]{2,1,0:T(8,128)} %get-tuple-element.48.eall, bf16[32,32,128]{2,1,0:T(8,128)(2,1)} %bitcast.56), custom_call_target="tpu_custom_call" | custom-call | tf_op jit(solution)/shard_map/pallas_call | solution.py:634
  84.2 10.4 %shard_map.249 = (bf16[128,1024]{1,0:T(8,128)(2,1)}, bf16[128,1024]{1,0:T(8,128)(2,1)}, bf16[128,1024]{1,0:T(8,128)(2,1)}, f32[8,128]{1,0:T(8,128)}, f32[8,128]{1,0:T(8,128)}, /*index=5*/f32[16,128]{1,0:T(8,128)}) custom-call(bf16[8,128,128]{2,1,0:T(8,128)(2,1)} %bitcast.44, bf16[8,128,128]{2,1,0:T(8,128)(2,1)} %bitcast.47, bf16[128,1024]{1,0:T(8,128)(2,1)} %bitcast.42, ...), custom_call_target="tpu_custom_call" | custom-call | tf_op jit(solution)/shard_map/pallas_call | solution.py:634
  94.6 0.0 all-gather.2.cloned.1.call-done.kv_ref
  94.6 46.8 %shard_map.250 = (bf16[128,2048]{1,0:T(8,128)(2,1)}, bf16[128,2048]{1,0:T(8,128)(2,1)}, bf16[128,2048]{1,0:T(8,128)(2,1)}, bf16[128,256]{1,0:T(8,128)(2,1)}, bf1...) custom-call(bf16[128,2048]{1,0:T(8,128)(2,1)} %bitcast.51, bf16[128,2048]{1,0:T(8,128)(2,1)} %bitcast.52, ...), custom_call_target="tpu_custom_call" | custom-call | tf_op jit(solution)/shard_map/pallas_call | solution.py:634
  141.4 1.3 slice_reduce_fusion
  142.7 1.2 slice_bitcast_fusion
  143.9 1.9 %copy.33 = bf16[1,128,2048]{2,1,0:T(8,128)(2,1)} copy(bf16[1,128,2048]{2,1,0:T(8,128)(2,1)} %bitcast.50) | data formatting | bytes 1048576
  145.7 1.9 %copy.34 = bf16[1,128,2048]{2,1,0:T(8,128)(2,1)} copy(bf16[1,128,2048]{2,1,0:T(8,128)(2,1)} %bitcast.49) | data formatting | bytes 1048576
  147.6 1.5 copy.35
  149.1 1.5 copy.36
  150.6 1.9 %copy.37 = bf16[1,128,2048]{2,1,0:T(8,128)(2,1)} copy(bf16[1,128,2048]{2,1,0:T(8,128)(2,1)} %bitcast.48) | data formatting | bytes 1048576
Async XLA Ops:
  7.2 87.4 %all-gather.2.cloned.1.call-start = ((), (), s32[]{:S(2)}) async-start(), calls=%async_computation | async-start | bytes 4325376 | tf_op jit(solution)/shard_map/all_gather | solution.py:665
Sparse Core Ops, SparseCore 0:
  10.3 54.4 all-gather.1

commit v3 on v2

v3 whole, which is shorter than its diff:
```python
import functools

import jax
import jax.numpy as jnp
from jax import lax
from jax.experimental import pallas as pl
from jax.experimental.pallas import tpu as pltpu
from jax.sharding import PartitionSpec as P

f32, bf16 = jnp.float32, jnp.bfloat16
MESH = pl.DeviceIdType.MESH
HIGHEST = lax.Precision.HIGHEST
NEG_FILL = -1e30
N = 32
C = 128
DK = 128
AD = 256
HEADS = 8
GROUP = 8
ROWS = GROUP * C
KB = 512
LENGTH = N * C
NKB = LENGTH // KB
QUARTERS = N // HEADS
SROWS = DK // QUARTERS
KEEP = 16
CHIPS = N // 2
VMEM_BIG = 60 * 1024 * 1024

NT = (((1,), (1,)), ((), ()))
NN = (((1,), (0,)), ((), ()))
TN = (((0,), (0,)), ((), ()))


def d1(a, b, dims):
    return lax.dot_general(a.astype(bf16), b.astype(bf16), dims, preferred_element_type=f32)


def split(a):
    hi = a.astype(bf16)
    return hi, (a - hi.astype(f32)).astype(bf16)


def d3(a, b, dims):
    ah, al = split(a)
    bh, bl = split(b)

    def dot(x, y):
        return lax.dot_general(x, y, dims, preferred_element_type=f32)

    return dot(ah, bh) + (dot(ah, bl) + dot(al, bh))


def dfull(a, b, dims):
    return lax.dot_general(a, b, dims, precision=HIGHEST, preferred_element_type=f32)


def iotas(shape=(C, C)):
    return (
        lax.broadcasted_iota(jnp.int32, shape, 0),
        lax.broadcasted_iota(jnp.int32, shape, 1),
    )


def unit(x):
    r = lax.rsqrt(jnp.sum(x * x, axis=-1, keepdims=True) + 1e-6)
    return x * r, r


def gates_of(bl_ref, di_ref, dl_ref):
    beta = 1.0 / (1.0 + jnp.exp(-bl_ref[...]))
    a = di_ref[...]
    head = lax.broadcasted_iota(jnp.int32, a.shape, 0)
    logs = jnp.zeros(a.shape, f32)
    for h in range(HEADS):
        logs = jnp.where(head == h, dl_ref[h], logs)
    rate = -jnp.exp(logs)
    soft = jnp.maximum(a, 0.0) + jnp.log1p(jnp.exp(-jnp.abs(a)))
    g = jnp.maximum(rate * soft, -104.0)
    r, c = iotas()
    beta_cols = dfull(jnp.where(r == c, 1.0, 0.0), beta, NT)
    cols = dfull(jnp.where(r >= c, 1.0, 0.0), g, NT)
    rows = dfull(g, jnp.where(r <= c, 1.0, 0.0), NN)
    return beta, g, rate, beta_cols, cols, rows


def fade(cc, cr):
    r, c = iotas()
    return jnp.where(r >= c, jnp.exp(jnp.where(r >= c, cc - cr, 0.0)), 0.0)


def head_cols(ref, h):
    return ref[:, h * DK : (h + 1) * DK].astype(f32)


def peers_of(me):
    core = lax.rem(me, 2)
    return me // 2, core, me + 1 - 2 * core


def remote(src, dst, send, recv, peer):
    if not isinstance(peer, dict):
        peer = {"ctx": peer}
    return pltpu.make_async_remote_copy(
        src_ref=src, dst_ref=dst, send_sem=send, recv_sem=recv, device_id=peer, device_id_type=MESH
    )


def whole_kernel(
    q_ref, k_ref, v_ref, bl_ref, di_ref, dl_ref, gain_ref, gate_ref, cot_ref,
    aq_ref, ak_ref, av_ref, ag_ref, ac_ref,
    out_ref, dq_ref, dk_ref, dv_ref, dbl_ref, ddi_ref, dgate_ref,
    aout_ref, adq_ref, adk_ref, adv_ref, adgate_ref, sums_ref,
    beta_s, cols_s, rows_s, n_ref, w_ref, u0_ref, u_ref, do_ref, dul_ref,
    m_ref, o_ref, mall, oall, eall, sbuf, srecv, l_ref, lall, tbuf, trecv,
    keys, values,
    qs, ups, probs, att, dqt, top, low, cent, block, keep, give, got, both, taken,
    x_ref, pairs, part, every, total, others,
    m_send, m_recv, f_send, f_recv, o_send, o_recv, s_send, s_recv, l_send, l_recv, t_send, t_recv,
    k_send, k_recv, kf_send, kf_recv, v_send, v_recv, vf_send, vf_recv,
    g_send, g_recv, b_send, b_recv, p_send, p_recv, e_send, e_recv, a_send, a_recv,
):
    me, head, section = (lax.axis_index(a) for a in ("ctx", "head", "section"))
    chip, core, mate = peers_of(me)
    barrier = pltpu.get_barrier_semaphore()
    turns = ((0, 1), (1, 0), (1, 1))

    def aside(i):
        dh, ds = turns[i]
        return {"head": lax.rem(head + dh, 2), "section": lax.rem(section + ds, 2)}

    def hello(p, carry):
        pl.semaphore_signal(
            barrier, inc=1, device_id={"ctx": lax.rem(me + p, N)}, device_id_type=MESH
        )
        return carry

    lax.fori_loop(1, N, hello, 0)
    for i in range(3):
        pl.semaphore_signal(barrier, inc=1, device_id=aside(i), device_id_type=MESH)

    r, c = iotas()
    beta_rows, g, rate, beta, cols, rows = gates_of(bl_ref, di_ref, dl_ref)
    beta_s[...] = beta
    cols_s[...] = cols
    rows_s[...] = rows

    def chunk(heads):
        ks = [unit(head_cols(k_ref, h))[0] for h in heads]
        lows = []
        for h, K in zip(heads, ks):
            F = fade(cols[:, h : h + 1], rows[h : h + 1, :])
            lows.append(jnp.where(r > c, beta[:, h : h + 1] * F * d1(K, K, NT), 0.0))
        inv = [
            jnp.where(r == c, 1.0, 0.0) - jnp.where(r // 2 == c // 2, L, 0.0) for L in lows
        ]
        k = 2
        while k < C:
            part_k = (r // (2 * k) == c // (2 * k)) & (r // k != c // k)
            mid = [d1(I, jnp.where(part_k, L, 0.0), NN) for I, L in zip(inv, lows)]
            inv = [I - d1(T, I, NN) for I, T in zip(inv, mid)]
            k *= 2
        for h, K, I in zip(heads, ks, inv):
            b, cc = beta[:, h : h + 1], cols[:, h : h + 1]
            V = head_cols(v_ref, h)
            W = d3(I, (b * jnp.exp(cc)) * K, NN)
            U0 = d3(I, b * V, NN)
            cl = cc[C - 1 : C, :]
            Kt = jnp.exp(cl - cc) * K
            n_ref[h] = I
            w_ref[h] = W
            u0_ref[h] = U0
            m_ref[h] = (-d3(W, Kt, TN)).astype(bf16)
            off = d3(U0, Kt, TN).astype(bf16)
            stay = jnp.broadcast_to(jnp.exp(cl), (KEEP, DK))
            high = stay.astype(bf16)
            mid = (stay - high.astype(f32)).astype(bf16)
            last = stay - high.astype(f32) - mid.astype(f32)
            row = lax.broadcasted_iota(jnp.int32, (KEEP, DK), 0)
            terms = jnp.where(row == 0, high.astype(f32), jnp.where(row == 1, mid.astype(f32), last))
            for q in range(QUARTERS):
                o_ref[h * QUARTERS + q, 0:SROWS, :] = off[q * SROWS : (q + 1) * SROWS, :]
                o_ref[h * QUARTERS + q, SROWS : SROWS + KEEP, :] = terms.astype(bf16)

    def map_copy(peer, source):
        return remote(
            m_ref.at[peer // QUARTERS], mall.at[source], m_send.at[peer // 2], m_recv.at[source], peer
        )

    def offset_copy(peer, source):
        return remote(o_ref.at[peer], oall.at[source], o_send.at[peer], o_recv.at[source], peer)

    half = CHIPS // 2
    for first in (0, 1):
        chunk(range(first * HEADS // 2, (first + 1) * HEADS // 2))
        if first == 0:
            pl.semaphore_wait(barrier, N + 2)

        def send_map(t, carry):
            to = first * half + lax.rem(chip + t, half)

            @pl.when(to != chip)
            def _():
                map_copy(2 * to + core, me).start()

            return carry

        def send_offset(t, carry):
            to = first * N // 2 + lax.rem(me + t, N // 2)

            @pl.when(to != me)
            def _():
                offset_copy(to, me).start()

            return carry

        lax.fori_loop(0, half, send_map, 0)
        lax.fori_loop(0, N // 2, send_offset, 0)
    mall[me] = m_ref[me // QUARTERS]
    oall[me] = o_ref[me]

    def map_pass(source):
        return remote(mall.at[source], mall.at[source], f_send.at[source], f_recv.at[source], mate)

    def state_copy(s, source):
        return remote(sbuf.at[s], srecv.at[source], s_send.at[s], s_recv.at[source], s)

    def arrive(cc):
        source = 2 * cc + core

        @pl.when(source != me)
        def _():
            map_copy(source, source).wait_recv()

        map_pass(source).start()

    def advance(s, S):
        @pl.when(s != me)
        def _():
            offset_copy(s, s).wait_recv()

        sbuf[s] = S.astype(bf16)

        @pl.when(s != me)
        def _():
            state_copy(s, me).start()

        terms = oall[s, SROWS : SROWS + KEEP, :].astype(f32)
        stay = terms[0:1] + (terms[1:2] + terms[2:3])
        eall[s] = jnp.broadcast_to(stay, (8, DK))
        return stay * S + d1(S, mall[s], NN) + oall[s, 0:SROWS, :].astype(f32)

    def pair(cc, S):
        map_pass(2 * cc + 1 - core).wait_recv()
        return advance(2 * cc + 1, advance(2 * cc, S))

    def forth(cc, S):
        arrive(cc)
        return pair(cc - 1, S)

    arrive(0)
    S_end = lax.fori_loop(1, CHIPS, forth, jnp.zeros((SROWS, DK), f32))
    pair(CHIPS - 1, S_end)
    srecv[me] = sbuf[me]

    def take_state(p, carry):
        peer = lax.rem(me + p, N)
        state_copy(peer, peer).wait_recv()
        return carry

    lax.fori_loop(1, N, take_state, 0)

    def own_rows(device):
        return pl.ds(pl.multiple_of(device * C, C), C)

    def wide_copy(ref, send, recv, to, source):
        at = own_rows(2 * source + core)
        return remote(ref.at[at, :], ref.at[at, :], send.at[to], recv.at[source], 2 * to + core)

    def wide_pass(ref, send, recv, which, source):
        at = own_rows(2 * source + which)
        return remote(ref.at[at, :], ref.at[at, :], send.at[source], recv.at[source], mate)

    def spread(own, ref, send, recv):
        ref[own_rows(me), :] = own[...]

        @pl.when(lax.rem(chip, 2) == 0)
        def _():
            ref[pl.ds(pl.multiple_of((chip + 1) * 2 * C, C), 2 * C), :] = jnp.zeros((2 * C, AD), bf16)

        def go(to, carry):
            wide_copy(ref, send, recv, to, chip).start()
            return carry

        lax.fori_loop(chip + 1, CHIPS, go, 0)

    def pass_on(ref, send, recv, pass_send, pass_recv):
        wide_pass(ref, pass_send, pass_recv, core, chip).start()

        def go(t, carry):
            source = chip - t
            wide_copy(ref, send, recv, source, source).wait_recv()
            wide_pass(ref, pass_send, pass_recv, core, source).start()
            return carry

        lax.fori_loop(1, chip + 1, go, 0)

    def complete(ref, pass_send, pass_recv):
        def go(source, carry):
            wide_pass(ref, pass_send, pass_recv, 1 - core, source).wait_recv()
            return carry

        lax.fori_loop(0, chip + 1, go, 0)

    spread(ak_ref, keys, k_send, k_recv)

    def slope_copy(peer, source):
        return remote(l_ref.at[peer], lall.at[source], l_send.at[peer], l_recv.at[source], peer)

    def state_of(ref, h):
        return ref[h * QUARTERS : (h + 1) * QUARTERS].reshape(DK, DK).astype(f32)

    gain = gain_ref[...]
    gain_sum = jnp.zeros((1, DK), f32)
    for h in range(HEADS):
        at = slice(h * DK, (h + 1) * DK)
        Q = unit(head_cols(q_ref, h))[0] * DK**-0.5
        K = unit(head_cols(k_ref, h))[0]
        S, W = state_of(srecv, h), w_ref[h]
        cc = cols_s[:, h : h + 1]
        ec = jnp.exp(cc)
        F = fade(cc, rows_s[h : h + 1, :])
        U = u0_ref[h] - d3(W, S, NT)
        Pm = d3(Q, K, NT) * F
        m = ec * d3(Q, S, NT) + d3(Pm, U, NN)
        rr = lax.rsqrt(jnp.mean(m * m, axis=-1, keepdims=True) + 1e-6)
        gate = head_cols(gate_ref, h)
        cot = head_cols(cot_ref, h)
        sig = 1.0 / (1.0 + jnp.exp(-gate))
        silu = gate * sig
        nm = m * rr
        out_ref[:, at] = (nm * gain * silu).astype(bf16)
        dgate_ref[:, at] = (cot * nm * gain * (sig * (1.0 + gate * (1.0 - sig)))).astype(bf16)
        gain_sum = gain_sum + jnp.sum(cot * nm * silu, axis=0, keepdims=True)
        dn = cot * gain * silu
        dO = rr * dn - m * (rr * rr * rr) * jnp.mean(m * dn, axis=-1, keepdims=True)
        dUl = d3(Pm, dO, TN)
        u_ref[h] = U
        do_ref[h] = dO
        dul_ref[h] = dUl
        slope = (d3(ec * dO, Q, TN) - d3(dUl, W, TN)).astype(bf16)
        for q in range(QUARTERS):
            l_ref[h * QUARTERS + q] = slope[q * SROWS : (q + 1) * SROWS, :]

    x_ref[HEADS : 2 * HEADS, :] = jnp.broadcast_to(gain_sum, (HEADS, DK))

    def send_slope(p, carry):
        slope_copy(lax.rem(me + p, N), me).start()
        return carry

    lax.fori_loop(1, N, send_slope, 0)
    lall[me] = l_ref[me]

    def turn_copy(s, source):
        return remote(tbuf.at[s], trecv.at[source], t_send.at[s], t_recv.at[source], s)

    def back(t, S):
        s = N - 1 - t
        tbuf[s] = S.astype(bf16)

        @pl.when(s != me)
        def _():
            turn_copy(s, me).start()
            slope_copy(s, s).wait_recv()

        return eall[s, 0:1, :] * S + d1(S, mall[s], NT) + lall[s].astype(f32)

    lax.fori_loop(0, N, back, jnp.zeros((SROWS, DK), f32))
    trecv[me] = tbuf[me]
    pass_on(keys, k_send, k_recv, kf_send, kf_recv)

    def take_turn(p, carry):
        peer = lax.rem(me + p, N)
        turn_copy(peer, peer).wait_recv()
        return carry

    lax.fori_loop(1, N, take_turn, 0)
    spread(av_ref, values, v_send, v_recv)

    lane = lax.broadcasted_iota(jnp.int32, (C, DK), 1)
    sub = lax.broadcasted_iota(jnp.int32, (HEADS, C), 0)
    dbeta = jnp.zeros((C, DK), f32)
    dcol = jnp.zeros((C, DK), f32)
    drow = jnp.zeros((HEADS, C), f32)
    dlast = jnp.zeros((HEADS, C), f32)
    for h in range(HEADS):
        at = slice(h * DK, (h + 1) * DK)
        xq, xk = head_cols(q_ref, h), head_cols(k_ref, h)
        Q0, rq = unit(xq)
        Q = Q0 * DK**-0.5
        K, rk = unit(xk)
        V = head_cols(v_ref, h)
        S, dS = state_of(srecv, h), state_of(trecv, h)
        I, U, dO, dUl = n_ref[h], u_ref[h], do_ref[h], dul_ref[h]
        b, cc = beta_s[:, h : h + 1], cols_s[:, h : h + 1]
        ec = jnp.exp(cc)
        F = fade(cc, rows_s[h : h + 1, :])
        cl = cc[C - 1 : C, :]
        tail = jnp.exp(cl - cc)
        A = d1(K, K, NT)
        QK = d3(Q, K, NT)
        dU = dUl + d3(tail * K, dS, NT)
        QS = ec * d3(Q, S, NT)
        Y = d3(K, S, NT)
        dPF = d3(dO, U, NT) * F
        dQ = ec * d3(dO, S, NN) + d3(dPF, K, NN)
        dKt = tail * d3(U, dS, NN)
        tau = jnp.sum(dKt * K, axis=-1, keepdims=True)
        dcl = jnp.sum(tau, axis=0, keepdims=True) + jnp.exp(cl) * jnp.sum(
            jnp.sum(dS * S, axis=-1, keepdims=True), axis=0, keepdims=True
        )
        dR = d3(I, dU, TN)
        dV = b * dR
        dY = (-ec) * dV
        dLF = jnp.where(r > c, -d3(dR, U, NT), 0.0) * F
        G2 = dLF * A
        db = jnp.sum(dR * (V - ec * Y), axis=-1, keepdims=True) + jnp.sum(
            G2, axis=-1, keepdims=True
        )
        dA = b * dLF
        dK = d3(dPF, Q, TN) + dKt + d3(dY, S, NN) + d3(dA, K, NN) + d3(dA, K, TN)
        G = dPF * QK + b * G2
        dcc = jnp.sum(dO * QS + dY * Y, axis=-1, keepdims=True) - tau + jnp.sum(
            G, axis=-1, keepdims=True
        )
        dbeta = jnp.where(lane == h, db, dbeta)
        dcol = jnp.where(lane == h, dcc, dcol)
        drow = jnp.where(sub == h, -jnp.sum(G, axis=0, keepdims=True), drow)
        dlast = jnp.where(sub == h, dcl, dlast)
        dq_ref[:, at] = (
            DK**-0.5 * (rq * dQ - xq * (rq * rq * rq) * jnp.sum(xq * dQ, axis=-1, keepdims=True))
        ).astype(bf16)
        dk_ref[:, at] = (
            rk * dK - xk * (rk * rk * rk) * jnp.sum(xk * dK, axis=-1, keepdims=True)
        ).astype(bf16)
        dv_ref[:, at] = dV.astype(bf16)
    since = jnp.where(r >= c, 1.0, 0.0)
    dg = dfull(dcol, since, TN)[:HEADS] + dfull(drow, since, NN) + dlast
    dbeta = dfull(dbeta, jnp.where(r == c, 1.0, 0.0), TN)[:HEADS]
    dbl_ref[...] = dbeta * beta_rows * (1.0 - beta_rows)
    ddi_ref[...] = dg * rate / (1.0 + jnp.exp(-di_ref[...]))
    x_ref[0:HEADS, :] = jnp.zeros((HEADS, DK), f32)
    x_ref[0:HEADS, 0:HEADS] = dfull(jnp.ones((HEADS, C), f32), dg * g, NT)

    def pair_copy():
        return remote(x_ref, pairs, p_send, p_recv, mate)

    def every_copy(p, source):
        peer = lax.rem(chip + p, CHIPS) * 2 + core
        return remote(part, every.at[source], e_send.at[p], e_recv.at[source], peer)

    def aside_copy(i):
        return remote(total, others.at[i], a_send.at[i], a_recv.at[i], aside(i))

    pair_copy().start()
    pass_on(values, v_send, v_recv, vf_send, vf_recv)
    blocks = me // (KB // C) + 1
    scale = AD**-0.5
    width = 256
    parts = ROWS // width
    for g in range(GROUP):
        qs[g * C : (g + 1) * C, :] = (
            aq_ref[:, g * AD : (g + 1) * AD].astype(f32) * scale
        ).astype(bf16)
    top[...] = jnp.full((8, ROWS), NEG_FILL, f32)
    low[...] = jnp.zeros((8, ROWS), f32)
    att[...] = jnp.zeros((AD, ROWS), f32)
    dqt[...] = jnp.zeros((AD, ROWS), f32)
    key_at, query_at = iotas((KB, width))
    reach = me * C + lax.rem(query_at, C) - key_at

    def rows_of(kb):
        return pl.ds(pl.multiple_of(kb * KB, KB), KB)

    def score(kb, carry):
        kblock = keys[rows_of(kb), :]
        for i in range(parts):
            cols = slice(i * width, (i + 1) * width)
            s = lax.dot_general(kblock, qs[cols, :], NT, preferred_element_type=f32)
            s = jnp.where(reach >= kb * KB, s, NEG_FILL)
            probs[rows_of(kb), cols] = s
            top[:, cols] = jnp.maximum(
                top[:, cols], jnp.max(s.reshape(KB // 8, 8, width), axis=0)
            )
        return carry

    complete(keys, kf_send, kf_recv)
    lax.fori_loop(0, blocks, score, 0)
    peak = jnp.max(top[...], axis=0, keepdims=True)
    top[...] = jnp.broadcast_to(peak, (8, ROWS))

    def weigh(kb, carry):
        vblock = values[rows_of(kb), :]
        for i in range(parts):
            cols = slice(i * width, (i + 1) * width)
            p = jnp.exp(probs[rows_of(kb), cols] - top[0:1, cols])
            probs[rows_of(kb), cols] = p
            low[:, cols] = low[:, cols] + jnp.sum(p.reshape(KB // 8, 8, width), axis=0)
            att[:, cols] = att[:, cols] + lax.dot_general(
                vblock, p.astype(bf16), TN, preferred_element_type=f32
            )
        return carry

    pair_copy().wait()
    part[...] = x_ref[...] + pairs[...]

    def send_part(p, carry):
        every_copy(p, chip).start()
        return carry

    lax.fori_loop(1, CHIPS, send_part, 0)
    every[chip] = part[...]
    complete(values, vf_send, vf_recv)
    lax.fori_loop(0, blocks, weigh, 0)
    share = 1.0 / jnp.sum(low[...], axis=0, keepdims=True)
    low[...] = jnp.broadcast_to(share, (8, ROWS))
    for g in range(GROUP):
        cols = slice(g * C, (g + 1) * C)
        at = slice(g * AD, (g + 1) * AD)
        attended = jnp.transpose(att[:, cols] * low[0:1, cols])
        opening = 1.0 / (1.0 + jnp.exp(-ag_ref[:, at].astype(f32)))
        cot = ac_ref[:, at].astype(f32)
        aout_ref[:, at] = (attended * opening).astype(bf16)
        up = (cot * opening).astype(bf16)
        ups[cols, :] = up
        adgate_ref[:, at] = (cot * attended * opening * (1.0 - opening)).astype(bf16)
        center = jnp.sum(jnp.transpose(up.astype(f32) * attended), axis=0, keepdims=True)
        cent[:, cols] = jnp.broadcast_to(center, (8, C))

    def give_copy(c):
        return remote(give.at[c], got.at[c], g_send.at[c], g_recv.at[c], mate)

    def both_copy(c, source):
        return remote(both.at[c], taken.at[source], b_send.at[c], b_recv.at[source], 2 * c + core)

    def grads(kb):
        kblock = keys[rows_of(kb), :]
        vblock = values[rows_of(kb), :]
        dk = jnp.zeros((KB, AD), f32)
        dv = jnp.zeros((KB, AD), f32)
        for i in range(parts):
            cols = slice(i * width, (i + 1) * width)
            p = probs[rows_of(kb), cols] * low[0:1, cols]
            dp = lax.dot_general(vblock, ups[cols, :], NT, preferred_element_type=f32)
            ds = (p * (dp - cent[0:1, cols])).astype(bf16)
            dv = dv + lax.dot_general(p.astype(bf16), ups[cols, :], NN, preferred_element_type=f32)
            dk = dk + lax.dot_general(ds, qs[cols, :], NN, preferred_element_type=f32)
            dqt[:, cols] = dqt[:, cols] + lax.dot_general(
                kblock, ds, TN, preferred_element_type=f32
            )
        block[:, 0:AD] = dk
        block[:, AD : 2 * AD] = dv
        for u in range(KB // (2 * C)):
            c = kb * (KB // (2 * C)) + u
            mine = pl.multiple_of((2 * u + core) * C, C)
            theirs = pl.multiple_of((2 * u + 1 - core) * C, C)
            keep[c] = block[pl.ds(mine, C), :]
            give[c] = block[pl.ds(theirs, C), :].astype(bf16)

            @pl.when(c <= chip)
            def _():
                give_copy(c).start()

    def forward(kb):
        for u in range(KB // (2 * C)):
            c = kb * (KB // (2 * C)) + u

            @pl.when(c <= chip)
            def _():
                give_copy(c).wait_recv()
                both[c] = (keep[c] + got[c].astype(f32)).astype(bf16)

            @pl.when(c < chip)
            def _():
                both_copy(c, chip).start()

    def later(t, carry):
        kb = blocks - 1 - t
        grads(kb)
        forward(kb + 1)
        return carry

    grads(blocks - 1)
    lax.fori_loop(1, blocks, later, 0)
    forward(0)

    def take_part(p, carry):
        source = lax.rem(chip + p, CHIPS)
        every_copy(p, chip).wait_send()
        every_copy(p, source).wait_recv()
        return carry

    lax.fori_loop(1, CHIPS, take_part, 0)
    total[...] = jnp.sum(every[...], axis=0)
    for i in range(3):
        aside_copy(i).start()

    for g in range(GROUP):
        cols = slice(g * C, (g + 1) * C)
        adq_ref[:, g * AD : (g + 1) * AD] = (jnp.transpose(dqt[:, cols]) * scale).astype(bf16)

    keep[chip] = keep[chip] + got[chip].astype(f32)

    def collect(t, carry):
        source = CHIPS - 1 - t
        both_copy(source, source).wait_recv()
        keep[chip] = keep[chip] + taken[source].astype(f32)
        return carry

    def sent(c, carry):
        give_copy(c).wait_send()

        @pl.when(c < chip)
        def _():
            both_copy(c, chip).wait_send()

        return carry

    lax.fori_loop(0, CHIPS - 1 - chip, collect, 0)
    adk_ref[...] = keep[chip, :, 0:AD].astype(bf16)
    adv_ref[...] = keep[chip, :, AD : 2 * AD].astype(bf16)
    lax.fori_loop(0, chip + 1, sent, 0)
    for i in range(3):
        aside_copy(i).wait()
    same = slice(0, HEADS)
    gain = slice(HEADS, 2 * HEADS)
    sums_ref[same, :] = total[same, :] + others[0, same, :]
    sums_ref[gain, :] = (total[gain, :] + others[0, gain, :]) + (
        others[1, gain, :] + others[2, gain, :]
    )

    def drain(p, carry):
        peer = lax.rem(me + p, N)
        offset_copy(peer, me).wait_send()
        state_copy(peer, me).wait_send()
        slope_copy(peer, me).wait_send()
        turn_copy(peer, me).wait_send()
        return carry

    def drain_map(p, carry):
        map_copy(lax.rem(chip + p, CHIPS) * 2 + core, me).wait_send()
        return carry

    def drain_pass(cc, carry):
        map_pass(2 * cc + core).wait_send()
        return carry

    def drain_wide(to, carry):
        wide_copy(keys, k_send, k_recv, to, chip).wait_send()
        wide_copy(values, v_send, v_recv, to, chip).wait_send()
        return carry

    def drain_wide_pass(source, carry):
        wide_pass(keys, kf_send, kf_recv, core, source).wait_send()
        wide_pass(values, vf_send, vf_recv, core, source).wait_send()
        return carry

    lax.fori_loop(1, N, drain, 0)
    lax.fori_loop(1, CHIPS, drain_map, 0)
    lax.fori_loop(0, CHIPS, drain_pass, 0)
    lax.fori_loop(chip + 1, CHIPS, drain_wide, 0)
    lax.fori_loop(0, chip + 1, drain_wide_pass, 0)


def place_kernel(count, sums_ref, *refs):
    ins, outs = refs[:count], refs[count : 2 * count]
    log_ref, gain_ref, sems = refs[2 * count :]
    copies = [pltpu.make_async_copy(a, b, sems.at[i]) for i, (a, b) in enumerate(zip(ins, outs))]
    for copy in copies:
        copy.start()
    log_ref[...] = sums_ref[0:1, 0:HEADS]
    gain_ref[...] = sums_ref[HEADS : HEADS + 1, :]
    for copy in copies:
        copy.wait()


VM = pl.BlockSpec(memory_space=pltpu.VMEM)
SM = pl.BlockSpec(memory_space=pltpu.SMEM)
ANY = pl.BlockSpec(memory_space=pl.ANY)


def per_device(
    delta_query, delta_key, delta_value, beta_logit, decay_input, decay_log, norm_gain,
    output_gate, delta_cotangent, attn_query, attn_key, attn_value, attn_gate, attn_cotangent,
):
    wide, flat, own = (C, HEADS * DK), (C, GROUP * AD), (C, AD)
    rows, pair = (HEADS, C), (2 * HEADS, DK)
    square, states = (HEADS, DK, DK), (N, SROWS, DK)
    loaded = (N, SROWS + KEEP, DK)
    blocks = (CHIPS, C, 2 * AD)
    args = (
        delta_query[0], delta_key[0], delta_value[0], beta_logit[0].T, decay_input[0].T, decay_log,
        norm_gain[None], output_gate[0], delta_cotangent[0],
        attn_query[0], attn_key[0], attn_value[0], attn_gate[0], attn_cotangent[0],
    )

    def vm(shape, dtype=f32):
        return pltpu.VMEM(shape, dtype)

    def dma(count):
        return pltpu.SemaphoreType.DMA((count,))

    one = pltpu.SemaphoreType.DMA
    shapes = [(wide, bf16)] * 4 + [(rows, f32)] * 2 + [(wide, bf16)]
    shapes += [(flat, bf16)] * 2 + [(own, bf16)] * 2 + [(flat, bf16), (pair, f32)]
    shapes = [jax.ShapeDtypeStruct(s, d) for s, d in shapes]
    results = pl.pallas_call(
        whole_kernel,
        out_shape=tuple(shapes),
        in_specs=[SM if x.ndim == 1 else VM for x in args],
        out_specs=tuple(VM for _ in shapes),
        scratch_shapes=[vm((C, HEADS)), vm((C, HEADS)), vm(rows)]
        + [vm(square)] * 6
        + [vm(square, bf16), vm(loaded, bf16), vm((N, DK, DK), bf16), vm(loaded, bf16)]
        + [vm((N, 8, DK))]
        + [vm(states, bf16)] * 6
        + [vm((LENGTH, AD), bf16)] * 2
        + [vm((ROWS, AD), bf16)] * 2
        + [vm((LENGTH, ROWS)), vm((AD, ROWS)), vm((AD, ROWS))]
        + [vm((8, ROWS))] * 3
        + [vm((KB, 2 * AD)), vm(blocks)]
        + [vm(blocks, bf16)] * 4
        + [vm(pair), vm(pair), vm(pair), vm((CHIPS,) + pair), vm(pair), vm((3,) + pair)]
        + [dma(N)] * 12
        + [dma(CHIPS)] * 12
        + [one, one]
        + [dma(CHIPS)] * 2
        + [dma(3)] * 2,
        compiler_params=pltpu.CompilerParams(
            vmem_limit_bytes=VMEM_BIG, collective_id=1, has_side_effects=True
        ),
    )(*args)
    results, sums = results[:-1], results[-1]
    count = len(results)
    *placed, log_grad, gain_grad = pl.pallas_call(
        functools.partial(place_kernel, count),
        out_shape=tuple(shapes[:-1])
        + (jax.ShapeDtypeStruct((1, HEADS), f32), jax.ShapeDtypeStruct((1, DK), f32)),
        in_specs=[VM] + [ANY] * count,
        out_specs=(VM,) * (count + 2),
        scratch_shapes=[dma(count)],
        compiler_params=pltpu.CompilerParams(vmem_limit_bytes=VMEM_BIG),
    )(sums, *results)
    out, dq, dk, dv, dbl, ddi, dgate, aout, adq, adk, adv, adgate = placed
    return (
        out[None], dq[None], dk[None], dv[None], dbl.T[None], ddi.T[None], log_grad[0], gain_grad[0],
        dgate[None], aout[None], adq[None], adk[None], adv[None], adgate[None],
    )


def solution(mesh):
    split3 = P("section", "ctx", "head")
    in_specs = (split3,) * 5 + (P("head"), P()) + (split3,) * 7
    out_specs = (split3,) * 6 + (P("head"), P()) + (split3,) * 6
    return jax.shard_map(
        per_device, mesh=mesh, in_specs=in_specs, out_specs=out_specs, check_vma=False
    )
```

time: 161 us -> 134 us (0.83)
  between operations: 14.1 us -> 0.82 us
  local copies, waits for them, and re-layouts: 11.1 us -> 0 us
    unnamed x5 -> x0, local copies, waits for them, and re-layouts: 8.58 us -> none
    pallas_call x6 -> x2, Pallas kernels: 133 us -> 132 us  [the longest x1 128 us: per_device(): pl.pallas_call(whole_kernel, out_shape=tuple(shapes), in_specs=[SM if x.n...]
  transfers between devices with their start and end apart: 1 -> 0, of which waited for: 0 -> 0; matrix products, arithmetic and copies ran while one was open for 0% -> 0% of each run, Pallas kernels for 54% -> 0%
where the time goes in v3:
time: 134 us; the launch traced here: 133 us
  Pallas kernels  132 us (99%)
    pallas_call x1, Pallas kernels, per_device(): pl.pallas_call(whole_kernel, out_shape=tuple(shapes), in_specs=[SM if x.n...  128 us
    pallas_call x1, Pallas kernels, per_device(): pl.pallas_call(functools.partial(place_kernel, count), out_shape=tuple(sh...  4.24 us

profile of v3, /device:TPU:0, one launch (start us, length us, event | category | flops | bytes accessed | tf_op | source)
XLA Modules:
  0.0 133.2 jit_solution(3517819685779374975)
XLA Ops:
  0.7 128.1 %shard_map.245 = (bf16[128,1024]{1,0:T(8,128)(2,1)}, bf16[128,1024]{1,0:T(8,128)(2,1)}, bf16[128,1024]{1,0:T(8,128)(2,1)}, bf16[128,1024]{1,0:T(8,128)(2,1)}, f3...) custom-call(bf16[128,1024]{1,0:T(8,128)(2,1)} %bitcast.38, ...), custom_call_target="tpu_custom_call" | custom-call | tf_op jit(solution)/shard_map/pallas_call | solution.py:717
  128.8 4.2 %shard_map.246 = (bf16[128,1024]{1,0:T(8,128)(2,1)}, bf16[128,1024]{1,0:T(8,128)(2,1)}, bf16[128,1024]{1,0:T(8,128)(2,1)}, bf16[128,1024]{1,0:T(8,128)(2,1)}, f3...) custom-call(f32[16,128]{1,0:T(8,128)} %get-tuple-element.41.sums_ref, ...), custom_call_target="tpu_custom_call" | custom-call | tf_op jit(solution)/shard_map/pallas_call | solution.py:745

commit v4 on v3

--- a/solution.py
+++ b/solution.py
@@ -140,10 +140,55 @@
         pl.semaphore_signal(barrier, inc=1, device_id=aside(i), device_id_type=MESH)
 
     r, c = iotas()
-    beta_rows, g, rate, beta, cols, rows = gates_of(bl_ref, di_ref, dl_ref)
+    beta_rows, decay, rate, beta, cols, rows = gates_of(bl_ref, di_ref, dl_ref)
     beta_s[...] = beta
     cols_s[...] = cols
     rows_s[...] = rows
+
+    def own_rows(device):
+        return pl.ds(pl.multiple_of(device * C, C), C)
+
+    def wide_copy(ref, send, recv, to, source):
+        at = own_rows(2 * source + core)
+        return remote(ref.at[at, :], ref.at[at, :], send.at[to], recv.at[source], 2 * to + core)
+
+    def wide_pass(ref, send, recv, which, source):
+        at = own_rows(2 * source + which)
+        return remote(ref.at[at, :], ref.at[at, :], send.at[source], recv.at[source], mate)
+
+    def spread(own, ref, send, recv):
+        ref[own_rows(me), :] = own[...]
+
+        @pl.when(lax.rem(chip, 2) == 0)
+        def _():
+            ref[pl.ds(pl.multiple_of((chip + 1) * 2 * C, C), 2 * C), :] = jnp.zeros((2 * C, AD), bf16)
+
+        def go(to, carry):
+            wide_copy(ref, send, recv, to, chip).start()
+            return carry
+
+        lax.fori_loop(chip + 1, CHIPS, go, 0)
+
+    def pass_on(ref, send, recv, pass_send, pass_recv):
+        wide_pass(ref, pass_send, pass_recv, core, chip).start()
+
+        def go(t, carry):
+            source = chip - t
+            wide_copy(ref, send, recv, source, source).wait_recv()
+            wide_pass(ref, pass_send, pass_recv, core, source).start()
+            return carry
+
+        lax.fori_loop(1, chip + 1, go, 0)
+
+    def complete(ref, pass_send, pass_recv):
+        def go(source, carry):
+            wide_pass(ref, pass_send, pass_recv, 1 - core, source).wait_recv()
+            return carry
+
+        lax.fori_loop(0, chip + 1, go, 0)
+
+    pl.semaphore_wait(barrier, N + 2)
+    spread(ak_ref, keys, k_send, k_recv)
 
     def chunk(heads):
         ks = [unit(head_cols(k_ref, h))[0] for h in heads]
@@ -193,9 +238,6 @@
     half = CHIPS // 2
     for first in (0, 1):
         chunk(range(first * HEADS // 2, (first + 1) * HEADS // 2))
-        if first == 0:
-            pl.semaphore_wait(barrier, N + 2)
-
         def send_map(t, carry):
             to = first * half + lax.rem(chip + t, half)
 
@@ -219,6 +261,7 @@
     mall[me] = m_ref[me // QUARTERS]
     oall[me] = o_ref[me]
 
+
     def map_pass(source):
         return remote(mall.at[source], mall.at[source], f_send.at[source], f_recv.at[source], mate)
 
@@ -263,56 +306,50 @@
     pair(CHIPS - 1, S_end)
     srecv[me] = sbuf[me]
 
+    spread(av_ref, values, v_send, v_recv)
+    pass_on(keys, k_send, k_recv, kf_send, kf_recv)
+
+    blocks = me // (KB // C) + 1
+    scale = AD**-0.5
+    width = 256
+    parts = ROWS // width
+    for g in range(GROUP):
+        qs[g * C : (g + 1) * C, :] = (
+            aq_ref[:, g * AD : (g + 1) * AD].astype(f32) * scale
+        ).astype(bf16)
+    top[...] = jnp.full((8, ROWS), NEG_FILL, f32)
+    low[...] = jnp.zeros((8, ROWS), f32)
+    att[...] = jnp.zeros((AD, ROWS), f32)
+    dqt[...] = jnp.zeros((AD, ROWS), f32)
+    key_at, query_at = iotas((KB, width))
+    reach = me * C + lax.rem(query_at, C) - key_at
+
+    def rows_of(kb):
+        return pl.ds(pl.multiple_of(kb * KB, KB), KB)
+
+    def score(kb, carry):
+        kblock = keys[rows_of(kb), :]
+        for i in range(parts):
+            cols = slice(i * width, (i + 1) * width)
+            s = lax.dot_general(kblock, qs[cols, :], NT, preferred_element_type=f32)
+            s = jnp.where(reach >= kb * KB, s, NEG_FILL)
+            probs[rows_of(kb), cols] = s
+            top[:, cols] = jnp.maximum(
+                top[:, cols], jnp.max(s.reshape(KB // 8, 8, width), axis=0)
+            )
+        return carry
+
+    complete(keys, kf_send, kf_recv)
+    lax.fori_loop(0, blocks, score, 0)
+    peak = jnp.max(top[...], axis=0, keepdims=True)
+    top[...] = jnp.broadcast_to(peak, (8, ROWS))
+
     def take_state(p, carry):
         peer = lax.rem(me + p, N)
         state_copy(peer, peer).wait_recv()
         return carry
 
     lax.fori_loop(1, N, take_state, 0)
-
-    def own_rows(device):
-        return pl.ds(pl.multiple_of(device * C, C), C)
-
-    def wide_copy(ref, send, recv, to, source):
-        at = own_rows(2 * source + core)
-        return remote(ref.at[at, :], ref.at[at, :], send.at[to], recv.at[source], 2 * to + core)
-
-    def wide_pass(ref, send, recv, which, source):
-        at = own_rows(2 * source + which)
-        return remote(ref.at[at, :], ref.at[at, :], send.at[source], recv.at[source], mate)
-
-    def spread(own, ref, send, recv):
-        ref[own_rows(me), :] = own[...]
-
-        @pl.when(lax.rem(chip, 2) == 0)
-        def _():
-            ref[pl.ds(pl.multiple_of((chip + 1) * 2 * C, C), 2 * C), :] = jnp.zeros((2 * C, AD), bf16)
-
-        def go(to, carry):
-            wide_copy(ref, send, recv, to, chip).start()
-            return carry
-
-        lax.fori_loop(chip + 1, CHIPS, go, 0)
-
-    def pass_on(ref, send, recv, pass_send, pass_recv):
-        wide_pass(ref, pass_send, pass_recv, core, chip).start()
-
-        def go(t, carry):
-            source = chip - t
-            wide_copy(ref, send, recv, source, source).wait_recv()
-            wide_pass(ref, pass_send, pass_recv, core, source).start()
-            return carry
-
-        lax.fori_loop(1, chip + 1, go, 0)
-
-    def complete(ref, pass_send, pass_recv):
-        def go(source, carry):
-            wide_pass(ref, pass_send, pass_recv, 1 - core, source).wait_recv()
-            return carry
-
-        lax.fori_loop(0, chip + 1, go, 0)
-
-    spread(ak_ref, keys, k_send, k_recv)
 
     def slope_copy(peer, source):
         return remote(l_ref.at[peer], lall.at[source], l_send.at[peer], l_recv.at[source], peer)
@@ -361,6 +398,22 @@
     lax.fori_loop(1, N, send_slope, 0)
     lall[me] = l_ref[me]
 
+    pass_on(values, v_send, v_recv, vf_send, vf_recv)
+    def weigh(kb, carry):
+        vblock = values[rows_of(kb), :]
+        for i in range(parts):
+            cols = slice(i * width, (i + 1) * width)
+            p = jnp.exp(probs[rows_of(kb), cols] - top[0:1, cols])
+            probs[rows_of(kb), cols] = p
+            low[:, cols] = low[:, cols] + jnp.sum(p.reshape(KB // 8, 8, width), axis=0)
+            att[:, cols] = att[:, cols] + lax.dot_general(
+                vblock, p.astype(bf16), TN, preferred_element_type=f32
+            )
+        return carry
+
+    complete(values, vf_send, vf_recv)
+    lax.fori_loop(0, blocks, weigh, 0)
+
     def turn_copy(s, source):
         return remote(tbuf.at[s], trecv.at[source], t_send.at[s], t_recv.at[source], s)
 
@@ -377,7 +430,77 @@
 
     lax.fori_loop(0, N, back, jnp.zeros((SROWS, DK), f32))
     trecv[me] = tbuf[me]
-    pass_on(keys, k_send, k_recv, kf_send, kf_recv)
+    share = 1.0 / jnp.sum(low[...], axis=0, keepdims=True)
+    low[...] = jnp.broadcast_to(share, (8, ROWS))
+    for g in range(GROUP):
+        cols = slice(g * C, (g + 1) * C)
+        at = slice(g * AD, (g + 1) * AD)
+        attended = jnp.transpose(att[:, cols] * low[0:1, cols])
+        opening = 1.0 / (1.0 + jnp.exp(-ag_ref[:, at].astype(f32)))
+        cot = ac_ref[:, at].astype(f32)
+        aout_ref[:, at] = (attended * opening).astype(bf16)
+        up = (cot * opening).astype(bf16)
+        ups[cols, :] = up
+        adgate_ref[:, at] = (cot * attended * opening * (1.0 - opening)).astype(bf16)
+        center = jnp.sum(jnp.transpose(up.astype(f32) * attended), axis=0, keepdims=True)
+        cent[:, cols] = jnp.broadcast_to(center, (8, C))
+
+    def give_copy(c):
+        return remote(give.at[c], got.at[c], g_send.at[c], g_recv.at[c], mate)
+
+    def both_copy(c, source):
+        return remote(both.at[c], taken.at[source], b_send.at[c], b_recv.at[source], 2 * c + core)
+
+    def grads(kb):
+        kblock = keys[rows_of(kb), :]
+        vblock = values[rows_of(kb), :]
+        dk = jnp.zeros((KB, AD), f32)
+        dv = jnp.zeros((KB, AD), f32)
+        for i in range(parts):
+            cols = slice(i * width, (i + 1) * width)
+            p = probs[rows_of(kb), cols] * low[0:1, cols]
+            dp = lax.dot_general(vblock, ups[cols, :], NT, preferred_element_type=f32)
+            ds = (p * (dp - cent[0:1, cols])).astype(bf16)
+            dv = dv + lax.dot_general(p.astype(bf16), ups[cols, :], NN, preferred_element_type=f32)
+            dk = dk + lax.dot_general(ds, qs[cols, :], NN, preferred_element_type=f32)
+            dqt[:, cols] = dqt[:, cols] + lax.dot_general(
+                kblock, ds, TN, preferred_element_type=f32
+            )
+        block[:, 0:AD] = dk
+        block[:, AD : 2 * AD] = dv
+        for u in range(KB // (2 * C)):
+            c = kb * (KB // (2 * C)) + u
+            mine = pl.multiple_of((2 * u + core) * C, C)
+            theirs = pl.multiple_of((2 * u + 1 - core) * C, C)
+            keep[c] = block[pl.ds(mine, C), :]
+            give[c] = block[pl.ds(theirs, C), :].astype(bf16)
+
+            @pl.when(c <= chip)
+            def _():
+                give_copy(c).start()
+
+    def forward(kb):
+        for u in range(KB // (2 * C)):
+            c = kb * (KB // (2 * C)) + u
+
+            @pl.when(c <= chip)
+            def _():
+                give_copy(c).wait_recv()
+                both[c] = (keep[c] + got[c].astype(f32)).astype(bf16)
+
+            @pl.when(c < chip)
+            def _():
+                both_copy(c, chip).start()
+
+    def later(t, carry):
+        kb = blocks - 1 - t
+        grads(kb)
+        forward(kb + 1)
+        return carry
+
+    grads(blocks - 1)
+    lax.fori_loop(1, blocks, later, 0)
+    forward(0)
 
     def take_turn(p, carry):
         peer = lax.rem(me + p, N)
@@ -385,8 +508,6 @@
         return carry
 
     lax.fori_loop(1, N, take_turn, 0)
-    spread(av_ref, values, v_send, v_recv)
-
     lane = lax.broadcasted_iota(jnp.int32, (C, DK), 1)
     sub = lax.broadcasted_iota(jnp.int32, (HEADS, C), 0)
     dbeta = jnp.zeros((C, DK), f32)
@@ -450,7 +571,7 @@
     dbl_ref[...] = dbeta * beta_rows * (1.0 - beta_rows)
     ddi_ref[...] = dg * rate / (1.0 + jnp.exp(-di_ref[...]))
     x_ref[0:HEADS, :] = jnp.zeros((HEADS, DK), f32)
-    x_ref[0:HEADS, 0:HEADS] = dfull(jnp.ones((HEADS, C), f32), dg * g, NT)
+    x_ref[0:HEADS, 0:HEADS] = dfull(jnp.ones((HEADS, C), f32), dg * decay, NT)
 
     def pair_copy():
         return remote(x_ref, pairs, p_send, p_recv, mate)
@@ -463,53 +584,9 @@
         return remote(total, others.at[i], a_send.at[i], a_recv.at[i], aside(i))
 
     pair_copy().start()
-    pass_on(values, v_send, v_recv, vf_send, vf_recv)
-    blocks = me // (KB // C) + 1
-    scale = AD**-0.5
-    width = 256
-    parts = ROWS // width
     for g in range(GROUP):
-        qs[g * C : (g + 1) * C, :] = (
-            aq_ref[:, g * AD : (g + 1) * AD].astype(f32) * scale
-        ).astype(bf16)
-    top[...] = jnp.full((8, ROWS), NEG_FILL, f32)
-    low[...] = jnp.zeros((8, ROWS), f32)
-    att[...] = jnp.zeros((AD, ROWS), f32)
-    dqt[...] = jnp.zeros((AD, ROWS), f32)
-    key_at, query_at = iotas((KB, width))
-    reach = me * C + lax.rem(query_at, C) - key_at
-
-    def rows_of(kb):
-        return pl.ds(pl.multiple_of(kb * KB, KB), KB)
-
-    def score(kb, carry):
-        kblock = keys[rows_of(kb), :]
-        for i in range(parts):
-            cols = slice(i * width, (i + 1) * width)
-            s = lax.dot_general(kblock, qs[cols, :], NT, preferred_element_type=f32)
-            s = jnp.where(reach >= kb * KB, s, NEG_FILL)
-            probs[rows_of(kb), cols] = s
-            top[:, cols] = jnp.maximum(
-                top[:, cols], jnp.max(s.reshape(KB // 8, 8, width), axis=0)
-            )
-        return carry
-
-    complete(keys, kf_send, kf_recv)
-    lax.fori_loop(0, blocks, score, 0)
-    peak = jnp.max(top[...], axis=0, keepdims=True)
-    top[...] = jnp.broadcast_to(peak, (8, ROWS))
-
-    def weigh(kb, carry):
-        vblock = values[rows_of(kb), :]
-        for i in range(parts):
-            cols = slice(i * width, (i + 1) * width)
-            p = jnp.exp(probs[rows_of(kb), cols] - top[0:1, cols])
-            probs[rows_of(kb), cols] = p
-            low[:, cols] = low[:, cols] + jnp.sum(p.reshape(KB // 8, 8, width), axis=0)
-            att[:, cols] = att[:, cols] + lax.dot_general(
-                vblock, p.astype(bf16), TN, preferred_element_type=f32
-            )
-        return carry
+        cols = slice(g * C, (g + 1) * C)
+        adq_ref[:, g * AD : (g + 1) * AD] = (jnp.transpose(dqt[:, cols]) * scale).astype(bf16)
 
     pair_copy().wait()
     part[...] = x_ref[...] + pairs[...]
@@ -520,80 +597,6 @@
 
     lax.fori_loop(1, CHIPS, send_part, 0)
     every[chip] = part[...]
-    complete(values, vf_send, vf_recv)
-    lax.fori_loop(0, blocks, weigh, 0)
-    share = 1.0 / jnp.sum(low[...], axis=0, keepdims=True)
-    low[...] = jnp.broadcast_to(share, (8, ROWS))
-    for g in range(GROUP):
-        cols = slice(g * C, (g + 1) * C)
-        at = slice(g * AD, (g + 1) * AD)
-        attended = jnp.transpose(att[:, cols] * low[0:1, cols])
-        opening = 1.0 / (1.0 + jnp.exp(-ag_ref[:, at].astype(f32)))
-        cot = ac_ref[:, at].astype(f32)
-        aout_ref[:, at] = (attended * opening).astype(bf16)
-        up = (cot * opening).astype(bf16)
-        ups[cols, :] = up
-        adgate_ref[:, at] = (cot * attended * opening * (1.0 - opening)).astype(bf16)
-        center = jnp.sum(jnp.transpose(up.astype(f32) * attended), axis=0, keepdims=True)
-        cent[:, cols] = jnp.broadcast_to(center, (8, C))
-
-    def give_copy(c):
-        return remote(give.at[c], got.at[c], g_send.at[c], g_recv.at[c], mate)
-
-    def both_copy(c, source):
-        return remote(both.at[c], taken.at[source], b_send.at[c], b_recv.at[source], 2 * c + core)
-
-    def grads(kb):
-        kblock = keys[rows_of(kb), :]
-        vblock = values[rows_of(kb), :]
-        dk = jnp.zeros((KB, AD), f32)
-        dv = jnp.zeros((KB, AD), f32)
-        for i in range(parts):
-            cols = slice(i * width, (i + 1) * width)
-            p = probs[rows_of(kb), cols] * low[0:1, cols]
-            dp = lax.dot_general(vblock, ups[cols, :], NT, preferred_element_type=f32)
-            ds = (p * (dp - cent[0:1, cols])).astype(bf16)
-            dv = dv + lax.dot_general(p.astype(bf16), ups[cols, :], NN, preferred_element_type=f32)
-            dk = dk + lax.dot_general(ds, qs[cols, :], NN, preferred_element_type=f32)
-            dqt[:, cols] = dqt[:, cols] + lax.dot_general(
-                kblock, ds, TN, preferred_element_type=f32
-            )
-        block[:, 0:AD] = dk
-        block[:, AD : 2 * AD] = dv
-        for u in range(KB // (2 * C)):
-            c = kb * (KB // (2 * C)) + u
-            mine = pl.multiple_of((2 * u + core) * C, C)
-            theirs = pl.multiple_of((2 * u + 1 - core) * C, C)
-            keep[c] = block[pl.ds(mine, C), :]
-            give[c] = block[pl.ds(theirs, C), :].astype(bf16)
-
-            @pl.when(c <= chip)
-            def _():
-                give_copy(c).start()
-
-    def forward(kb):
-        for u in range(KB // (2 * C)):
-            c = kb * (KB // (2 * C)) + u
-
-            @pl.when(c <= chip)
-            def _():
-                give_copy(c).wait_recv()
-                both[c] = (keep[c] + got[c].astype(f32)).astype(bf16)
-
-            @pl.when(c < chip)
-            def _():
-                both_copy(c, chip).start()
-
-    def later(t, carry):
-        kb = blocks - 1 - t
-        grads(kb)
-        forward(kb + 1)
-        return carry
-
-    grads(blocks - 1)
-    lax.fori_loop(1, blocks, later, 0)
-    forward(0)
-
     def take_part(p, carry):
         source = lax.rem(chip + p, CHIPS)
         every_copy(p, chip).wait_send()
@@ -605,14 +608,11 @@
     for i in range(3):
         aside_copy(i).start()
 
-    for g in range(GROUP):
-        cols = slice(g * C, (g + 1) * C)
-        adq_ref[:, g * AD : (g + 1) * AD] = (jnp.transpose(dqt[:, cols]) * scale).astype(bf16)
 
     keep[chip] = keep[chip] + got[chip].astype(f32)
 
     def collect(t, carry):
-        source = CHIPS - 1 - t
+        source = chip + 1 + t
         both_copy(source, source).wait_recv()
         keep[chip] = keep[chip] + taken[source].astype(f32)
         return carry

time: 134 us -> 124 us (0.925)
  Pallas kernels: 132 us -> 123 us
    pallas_call x1, Pallas kernels: 128 us -> 119 us  [per_device(): pl.pallas_call(whole_kernel, out_shape=tuple(shapes), in_specs=[SM if x.n...]
where the time goes in v4:
time: 124 us
  Pallas kernels  123 us (99%)
    pallas_call x1, Pallas kernels, per_device(): pl.pallas_call(whole_kernel, out_shape=tuple(shapes), in_specs=[SM if x.n...  119 us
    pallas_call x1, Pallas kernels, per_device(): pl.pallas_call(functools.partial(place_kernel, count), out_shape=tuple(sh...  4.24 us

profile of v4, /device:TPU:0, one launch (start us, length us, event | category | flops | bytes accessed | tf_op | source)
XLA Modules:
  0.0 124.2 jit_solution(388619822382694114)
XLA Ops:
  0.7 119.2 %shard_map.245 = (bf16[128,1024]{1,0:T(8,128)(2,1)}, bf16[128,1024]{1,0:T(8,128)(2,1)}, bf16[128,1024]{1,0:T(8,128)(2,1)}, bf16[128,1024]{1,0:T(8,128)(2,1)}, f3...) custom-call(bf16[128,1024]{1,0:T(8,128)(2,1)} %bitcast.38, ...), custom_call_target="tpu_custom_call" | custom-call | tf_op jit(solution)/shard_map/pallas_call | solution.py:717
  119.8 4.2 %shard_map.246 = (bf16[128,1024]{1,0:T(8,128)(2,1)}, bf16[128,1024]{1,0:T(8,128)(2,1)}, bf16[128,1024]{1,0:T(8,128)(2,1)}, bf16[128,1024]{1,0:T(8,128)(2,1)}, f3...) custom-call(f32[16,128]{1,0:T(8,128)} %get-tuple-element.41.sums_ref, ...), custom_call_target="tpu_custom_call" | custom-call | tf_op jit(solution)/shard_map/pallas_call | solution.py:745

commit v5 on v4

--- a/solution.py
+++ b/solution.py
@@ -108,9 +108,11 @@
 
 def whole_kernel(
     q_ref, k_ref, v_ref, bl_ref, di_ref, dl_ref, gain_ref, gate_ref, cot_ref,
-    aq_ref, ak_ref, av_ref, ag_ref, ac_ref,
-    out_ref, dq_ref, dk_ref, dv_ref, dbl_ref, ddi_ref, dgate_ref,
-    aout_ref, adq_ref, adk_ref, adv_ref, adgate_ref, sums_ref,
+    aq_hbm, ak_ref, av_ref, ag_hbm, ac_hbm,
+    out_hbm, dq_hbm, dk_hbm, dv_hbm, dbl_ref, ddi_ref, dgate_hbm,
+    aout_hbm, adq_hbm, adk_ref, adv_ref, adgate_hbm, sums_ref,
+    aq_ref, ag_ref, ac_ref, out_ref, dq_ref, dk_ref, dv_ref, dgate_ref, aout_ref, adq_ref, adgate_ref,
+    load, store,
     beta_s, cols_s, rows_s, n_ref, w_ref, u0_ref, u_ref, do_ref, dul_ref,
     m_ref, o_ref, mall, oall, eall, sbuf, srecv, l_ref, lall, tbuf, trecv,
     keys, values,
@@ -123,6 +125,10 @@
     me, head, section = (lax.axis_index(a) for a in ("ctx", "head", "section"))
     chip, core, mate = peers_of(me)
     barrier = pltpu.get_barrier_semaphore()
+    ahead = ((aq_hbm, aq_ref), (ag_hbm, ag_ref), (ac_hbm, ac_ref))
+    loads = [pltpu.make_async_copy(a, b, load.at[i]) for i, (a, b) in enumerate(ahead)]
+    for copy in loads:
+        copy.start()
     turns = ((0, 1), (1, 0), (1, 1))
 
     def aside(i):
@@ -309,6 +315,8 @@
     spread(av_ref, values, v_send, v_recv)
     pass_on(keys, k_send, k_recv, kf_send, kf_recv)
 
+    for copy in loads:
+        copy.wait()
     blocks = me // (KB // C) + 1
     scale = AD**-0.5
     width = 256
@@ -588,6 +596,13 @@
         cols = slice(g * C, (g + 1) * C)
         adq_ref[:, g * AD : (g + 1) * AD] = (jnp.transpose(dqt[:, cols]) * scale).astype(bf16)
 
+    behind = (
+        (out_ref, out_hbm), (dq_ref, dq_hbm), (dk_ref, dk_hbm), (dv_ref, dv_hbm),
+        (dgate_ref, dgate_hbm), (aout_ref, aout_hbm), (adq_ref, adq_hbm), (adgate_ref, adgate_hbm),
+    )
+    stores = [pltpu.make_async_copy(a, b, store.at[i]) for i, (a, b) in enumerate(behind)]
+    for copy in stores:
+        copy.start()
     pair_copy().wait()
     part[...] = x_ref[...] + pairs[...]
 
@@ -670,17 +685,24 @@
     lax.fori_loop(0, CHIPS, drain_pass, 0)
     lax.fori_loop(chip + 1, CHIPS, drain_wide, 0)
     lax.fori_loop(0, chip + 1, drain_wide_pass, 0)
+    for copy in stores:
+        copy.wait()
 
 
 def place_kernel(count, sums_ref, *refs):
     ins, outs = refs[:count], refs[count : 2 * count]
-    log_ref, gain_ref, sems = refs[2 * count :]
-    copies = [pltpu.make_async_copy(a, b, sems.at[i]) for i, (a, b) in enumerate(zip(ins, outs))]
-    for copy in copies:
+    log_ref, gain_ref = refs[2 * count : 2 * count + 2]
+    held, sems = refs[2 * count + 2 : 3 * count + 2], refs[3 * count + 2]
+    first = [pltpu.make_async_copy(a, b, sems.at[0, i]) for i, (a, b) in enumerate(zip(ins, held))]
+    second = [pltpu.make_async_copy(a, b, sems.at[1, i]) for i, (a, b) in enumerate(zip(held, outs))]
+    for copy in first:
         copy.start()
     log_ref[...] = sums_ref[0:1, 0:HEADS]
     gain_ref[...] = sums_ref[HEADS : HEADS + 1, :]
-    for copy in copies:
+    for arrives, leaves in zip(first, second):
+        arrives.wait()
+        leaves.start()
+    for copy in second:
         copy.wait()
 
 
@@ -717,9 +739,13 @@
     results = pl.pallas_call(
         whole_kernel,
         out_shape=tuple(shapes),
-        in_specs=[SM if x.ndim == 1 else VM for x in args],
-        out_specs=tuple(VM for _ in shapes),
-        scratch_shapes=[vm((C, HEADS)), vm((C, HEADS)), vm(rows)]
+        in_specs=[ANY if i in (9, 12, 13) else SM if x.ndim == 1 else VM for i, x in enumerate(args)],
+        out_specs=tuple(ANY if i in (0, 1, 2, 3, 6, 7, 8, 11) else VM for i in range(len(shapes))),
+        scratch_shapes=[vm(flat, bf16)] * 3
+        + [vm(wide, bf16)] * 5
+        + [vm(flat, bf16)] * 3
+        + [dma(3), dma(8)]
+        + [vm((C, HEADS)), vm((C, HEADS)), vm(rows)]
         + [vm(square)] * 6
         + [vm(square, bf16), vm(loaded, bf16), vm((N, DK, DK), bf16), vm(loaded, bf16)]
         + [vm((N, 8, DK))]
@@ -747,8 +773,9 @@
         out_shape=tuple(shapes[:-1])
         + (jax.ShapeDtypeStruct((1, HEADS), f32), jax.ShapeDtypeStruct((1, DK), f32)),
         in_specs=[VM] + [ANY] * count,
-        out_specs=(VM,) * (count + 2),
-        scratch_shapes=[dma(count)],
+        out_specs=(ANY,) * count + (VM, VM),
+        scratch_shapes=[vm(x.shape, x.dtype) for x in results]
+        + [pltpu.SemaphoreType.DMA((2, count))],
         compiler_params=pltpu.CompilerParams(vmem_limit_bytes=VMEM_BIG),
     )(sums, *results)
     out, dq, dk, dv, dbl, ddi, dgate, aout, adq, adk, adv, adgate = placed

time: 124 us -> 123 us (level)
    pallas_call x1, Pallas kernels: 119 us -> 118 us  [per_device(): pl.pallas_call(whole_kernel, out_shape=tuple(shapes), in_specs=[ANY if i...]
where the time goes in v5:
time: 123 us
  Pallas kernels  122 us (99%)
    pallas_call x1, Pallas kernels, per_device(): pl.pallas_call(whole_kernel, out_shape=tuple(shapes), in_specs=[ANY if i...  118 us
    pallas_call x1, Pallas kernels, per_device(): pl.pallas_call(functools.partial(place_kernel, count), out_shape=tuple(sh...  4.07 us

profile of v5, /device:TPU:0, one launch (start us, length us, event | category | flops | bytes accessed | tf_op | source)
XLA Modules:
  0.0 122.7 jit_solution(8810731209879062714)
XLA Ops:
  0.7 117.9 %shard_map.245 = (bf16[128,1024]{1,0:T(8,128)(2,1)}, bf16[128,1024]{1,0:T(8,128)(2,1)}, bf16[128,1024]{1,0:T(8,128)(2,1)}, bf16[128,1024]{1,0:T(8,128)(2,1)}, f3...) custom-call(bf16[128,1024]{1,0:T(8,128)(2,1)} %bitcast.38, ...), custom_call_target="tpu_custom_call" | custom-call | tf_op jit(solution)/shard_map/pallas_call | solution.py:739
  118.5 4.1 %shard_map.246 = (bf16[128,1024]{1,0:T(8,128)(2,1)}, bf16[128,1024]{1,0:T(8,128)(2,1)}, bf16[128,1024]{1,0:T(8,128)(2,1)}, bf16[128,1024]{1,0:T(8,128)(2,1)}, f3...) custom-call(f32[16,128]{1,0:T(8,128)} %get-tuple-element.41.sums_ref, ...), custom_call_target="tpu_custom_call" | custom-call | tf_op jit(solution)/shard_map/pallas_call | solution.py:771
